TPU v7x, 32 devices: a whole 2x2x4 slice. The times are simulated.
32 devices in a mesh: scen: 4 (over y, core), row: 8 (over z, x).
Axes of the slice: x: 2, y: 2, z: 4, core: 2. Of those that a mesh axis runs over, the one named last changes fastest.
Arguments:
- borders: bfloat16 [4, 1024, 12288], P('scen', None, 'row'), may hold values from -1.078125 to 1.078125
- kkt_inverse: bfloat16 [4, 1024, 1024], P('scen', 'row'), may hold values from -0.35 to 2.35, as said below
- first_section: float32 [12288, 256], P('row'), may hold values from -6 to 6
- barrier: float32 [12288], P('row'), may hold values from 64 to 512
- panel_vars: int32 [256], replicated, may hold values from 0 to 12287, as said below
- probability: float32 [4], replicated, may hold values from 0.5 to 2
- assignment: int32 [4], P('scen'), may hold values from 0 to 3, each once
Outputs:
- factor: float32 [12288, 256], P('row')
Inputs may be any that keep to these rules, and one draw needn't show every extreme that they name: `panel_vars`: distinct values. `kkt_inverse`: each scenario's matrix is symmetric positive definite. `assignment`: each scenario once.
All inputs are finite; a program needn't handle non-finite values.
Results may differ from a plain program's by a relative error of at most 0.00031.
Values may be sent and summed in bfloat16 or wider, within the bound.
A program may use at most 64 MiB of HBM per device.

v0:
```python
import functools

import jax
import jax.numpy as jnp
from jax import lax
from jax.experimental import pallas as pl
from jax.experimental.pallas import tpu as pltpu
from jax.sharding import PartitionSpec as P

PANEL = 128
MESH = pl.DeviceIdType.MESH
HIGH = lax.Precision.HIGHEST
F32 = jnp.float32
BF16 = jnp.bfloat16
CHUNKS = 6
SUB = 8
BLOCK = 32


def small_factor(tile, first):
    shape = tile.shape
    spread = [
        jnp.broadcast_to(tile[:, first + k:first + k + 1], shape) for k in range(SUB)
    ]
    cell = {
        (i, k): jnp.broadcast_to(spread[k][i:i + 1, :], shape)
        for k in range(SUB) for i in range(k, SUB)
    }
    scale, lower = [], {}
    for j in range(SUB):
        scale.append(lax.rsqrt(cell[j, j]))
        for i in range(j + 1, SUB):
            lower[i, j] = cell[i, j] * scale[j]
        for k in range(j + 1, SUB):
            for i in range(k, SUB):
                cell[i, k] = cell[i, k] - lower[i, j] * lower[k, j]
    inverse = {}
    for j in range(SUB):
        inverse[j, j] = scale[j]
        for i in range(j + 1, SUB):
            total = lower[i, j] * inverse[j, j]
            for m in range(j + 1, i):
                total = total + lower[i, m] * inverse[m, j]
            inverse[i, j] = -(scale[i] * total)
    return inverse


def panel_inverse(block, size):
    panel = block.shape[0]
    shape = (SUB, panel)
    sub = lax.broadcasted_iota(jnp.int32, shape, 0)
    lane = lax.broadcasted_iota(jnp.int32, shape, 1)
    tiles = panel // SUB
    left = [block[low:low + SUB, :] for low in range(0, panel, SUB)]
    right = [jnp.where(lane == sub + low, 1.0, 0.0) for low in range(0, panel, SUB)]
    per = size // SUB
    for base in range(0, tiles, per):
        for own in range(base, base + per):
            first = own * SUB
            inverse = small_factor(left[own], first)
            new_left = new_right = None
            for k in range(SUB):
                coeff = inverse[SUB - 1, k]
                for i in range(SUB - 2, k - 1, -1):
                    coeff = jnp.where(sub <= i, inverse[i, k], coeff)
                if k:
                    coeff = jnp.where(sub < k, 0.0, coeff)
                add_left = coeff * left[own][k:k + 1, :]
                add_right = coeff * right[own][k:k + 1, :]
                new_left = add_left if k == 0 else new_left + add_left
                new_right = add_right if k == 0 else new_right + add_right
            for tile in range(own + 1, base + per):
                spread = [
                    jnp.broadcast_to(left[tile][:, first + m:first + m + 1], shape)
                    for m in range(SUB)
                ]
                for k in range(SUB):
                    factor = spread[0] * inverse[k, 0]
                    for m in range(1, k + 1):
                        factor = factor + spread[m] * inverse[k, m]
                    left[tile] = left[tile] - factor * new_left[k:k + 1, :]
                    right[tile] = right[tile] - factor * new_right[k:k + 1, :]
            left[own], right[own] = new_left, new_right
        if base + per < tiles:
            upper = jnp.concatenate(left[base:base + per], axis=0)
            both = jnp.concatenate(
                [upper, jnp.concatenate(right[base:base + per], axis=0)], axis=1
            )
            change = lax.dot_general(
                upper, both, (((0,), (0,)), ((), ())),
                precision=HIGH, preferred_element_type=F32,
            )
            for tile in range(base + per, tiles):
                low = tile * SUB
                left[tile] = left[tile] - change[low:low + SUB, :panel]
                right[tile] = right[tile] - change[low:low + SUB, panel:]
    return jnp.concatenate(right, axis=0)


def flip(index, bit):
    return index + bit * (1 - 2 * ((index // bit) % 2))


def toggle(index, mask):
    bit = 1
    while bit <= mask:
        if mask & bit:
            index = flip(index, bit)
        bit *= 2
    return index


def bits_down(count):
    bits = []
    bit = count // 2
    while bit >= 1:
        bits.append(bit)
        bit //= 2
    return bits


def low_bit(mask):
    return mask & -mask


def gather_blocks(arrays, me, count):
    bits = bits_down(count)

    def copy(array, owner, mask, bit):
        held, send_sem, recv_sem = array
        return pltpu.make_async_remote_copy(
            src_ref=held.at[owner],
            dst_ref=held.at[owner],
            send_sem=send_sem.at[mask],
            recv_sem=recv_sem.at[mask],
            device_id={"row": flip(me, bit)},
            device_id_type=MESH,
        )

    order = [0]
    for bit in bits:
        order += [mask + bit for mask in list(order)]
    sent = []
    for mask in order:
        for array in arrays:
            owner = toggle(me, mask)
            if mask:
                copy(array, owner, mask, low_bit(mask)).wait_recv()
            for bit in bits:
                if mask == 0 or bit < low_bit(mask):
                    one = copy(array, owner, mask + bit, bit)
                    one.start()
                    sent.append(one)
    return sent


def schur_kernel(
    n_scen, n_row,
    pv_row, prob, asg, bar_row, b_hbm, k_hbm, base_hbm,
    h_ref, m_ref,
    b_ref, k_ref, base, load_sem, rest_sem, pv_col, onehot, picked, parts, columns, solved, fpick, fparts, fall, bt,
    t_own, t_in, t_sum, t_all, out_half, in_half, mine, y_in,
    rs_send, rs_recv, fs_send, fs_recv, agc_send, agc_recv, agf_send, agf_recv,
    ags_send, ags_recv, t_send, t_recv, c_send, c_recv, y_send, y_recv,
    g_send, g_recv,
):
    scen = lax.axis_index("scen")
    row = lax.axis_index("row")
    depth = picked.shape[1]
    rows, window = base.shape
    barrier = pltpu.get_barrier_semaphore()

    def load(block):
        start = pl.multiple_of(block * depth, depth)
        return pltpu.make_async_copy(
            b_hbm.at[pl.ds(start, depth), :],
            b_ref.at[pl.ds(start, depth), :],
            load_sem.at[block],
        )

    base_load = pltpu.make_async_copy(base_hbm, base, rest_sem.at[0])
    k_load = pltpu.make_async_copy(k_hbm, k_ref, rest_sem.at[1])
    scen_bits = bits_down(n_scen)[::-1]
    for step in range(1, n_row):
        pl.semaphore_signal(
            barrier, inc=1, device_id={"row": (row + step) % n_row}, device_id_type=MESH
        )
    for bit in scen_bits:
        pl.semaphore_signal(
            barrier, inc=1, device_id={"scen": flip(scen, bit)}, device_id_type=MESH
        )

    for step in range(1, n_row + 1):
        load((row + step) % n_row).start()
    base_load.start()
    k_load.start()

    first = row * rows
    local = pv_row[...] - first
    onehot[...] = jnp.where(
        lax.broadcasted_iota(jnp.int32, (rows, window), 0) == local, 1.0, 0.0
    ).astype(BF16)

    frows = fpick.shape[0] * fpick.shape[1]
    groups = window // frows
    fstart = pl.multiple_of((scen % groups) * frows, 8)
    pv_col[...] = jnp.broadcast_to(pv_row[...], (SUB, window)).T
    flocal = pv_col[pl.ds(fstart, frows), 0:1] - first
    fhot = jnp.where(
        lax.broadcasted_iota(jnp.int32, (frows, rows), 1) == flocal, 1.0, 0.0
    ).astype(F32)

    pl.semaphore_wait(barrier, n_row - 1 + len(scen_bits))

    def pick(dst):
        load(dst).wait()
        start = pl.multiple_of(dst * depth, depth)
        block = jnp.dot(
            b_ref[pl.ds(start, depth), :], onehot[...], preferred_element_type=F32
        )
        return block.astype(BF16)

    def rs_copy(src, dst_ref, send, recv, dst, slot_send, slot_recv):
        return pltpu.make_async_remote_copy(
            src_ref=src,
            dst_ref=dst_ref,
            send_sem=send.at[slot_send],
            recv_sem=recv.at[slot_recv],
            device_id={"row": dst},
            device_id_type=MESH,
        )

    def send_pick(step, carry):
        dst = (row + step) % n_row
        picked[dst] = pick(dst)
        rs_copy(picked.at[dst], parts.at[row], rs_send, rs_recv, dst, dst, row).start()
        return carry

    lax.fori_loop(1, n_row, send_pick, 0)
    parts[row] = pick(row)

    bsel = jnp.dot(
        jnp.broadcast_to(bar_row[...].reshape(1, rows), (SUB, rows)), onehot[...].astype(F32),
        preferred_element_type=F32, precision=HIGH,
    )[0:1, :]
    slot_row = lax.broadcasted_iota(jnp.int32, (frows, window), 0) + fstart
    slot_col = lax.broadcasted_iota(jnp.int32, (frows, window), 1)
    base_load.wait()
    fpick[...] = (
        jnp.dot(fhot, base[...], preferred_element_type=F32, precision=HIGH)
        + jnp.where(slot_row == slot_col, bsel, 0.0)
    ).reshape(fpick.shape)
    for step in range(1, n_row):
        dst = (row + step) % n_row
        rs_copy(fpick.at[dst], fparts.at[row], fs_send, fs_recv, dst, dst, row).start()
    fparts[row] = fpick[row]

    def turn(tile, carry):
        start = pl.multiple_of(tile * PANEL, PANEL)
        bt[pl.ds(start, PANEL), :] = b_ref[:, pl.ds(start, PANEL)].T
        return carry

    lax.fori_loop(0, rows // PANEL, turn, 0)

    for step in range(1, n_row):
        src = (row + n_row - step) % n_row
        rs_copy(picked.at[src], parts.at[src], rs_send, rs_recv, src, src, src).wait_recv()
    total = parts[0].astype(F32)
    for slot in range(1, n_row):
        total = total + parts[slot].astype(F32)
    columns[row] = total.astype(BF16)
    for step in range(1, n_row):
        src = (row + n_row - step) % n_row
        rs_copy(fpick.at[src], fparts.at[src], fs_send, fs_recv, src, src, src).wait_recv()
    ftotal = fparts[0]
    for slot in range(1, n_row):
        ftotal = ftotal + fparts[slot]
    fall[row] = ftotal
    sent = gather_blocks(
        [(columns, agc_send, agc_recv), (fall, agf_send, agf_recv)], row, n_row
    )

    k_load.wait()
    own = jnp.dot(
        k_ref[...],
        columns[...].reshape(n_row * depth, window),
        preferred_element_type=F32,
    )
    solved[row] = own.astype(BF16)
    sent += gather_blocks([(solved, ags_send, ags_recv)], row, n_row)


    match = lax.broadcasted_iota(jnp.int32, prob.shape, 1) == asg[...]
    weight = jnp.sum(jnp.where(match, prob[...], 0.0), axis=1, keepdims=True)

    t_own[...] = weight * lax.dot_general(
        columns[...].reshape(n_row * depth, window),
        solved[...].reshape(n_row * depth, window),
        (((0,), (0,)), ((), ())),
        preferred_element_type=F32,
    )
    keep = jnp.where(scen < groups, 1.0, 0.0)
    t_own[pl.ds(fstart, frows), :] += fall[...].reshape(frows, window) * keep

    core = scen % 2
    t_half = window // 2
    t_mine = pl.multiple_of(core * t_half, 8)
    t_other = pl.multiple_of((1 - core) * t_half, 8)

    def t_copy(index):
        if index == 0:
            src, dst = t_own.at[pl.ds(t_other, t_half), :], t_in.at[0]
        elif index < len(scen_bits):
            src, dst = t_sum.at[index - 1], t_in.at[index]
        else:
            src = t_sum.at[index - 1]
            dst = t_all.at[pl.ds(t_mine, t_half), :]
        return pltpu.make_async_remote_copy(
            src_ref=src,
            dst_ref=dst,
            send_sem=t_send.at[index],
            recv_sem=t_recv.at[index],
            device_id={"scen": flip(scen, (scen_bits + [1])[index])},
            device_id_type=MESH,
        )

    t_copy(0).start()

    half = rows // 2
    chunk = half // CHUNKS
    def term(which, part):
        start = pl.multiple_of(which * half + part * chunk, 8)
        return weight * jnp.dot(
            bt[pl.ds(start, chunk), :],
            solved[...].reshape(n_row * depth, window),
            preferred_element_type=F32,
        )

    def c_copy(part):
        return pltpu.make_async_remote_copy(
            src_ref=out_half.at[part],
            dst_ref=in_half.at[part],
            send_sem=c_send.at[part],
            recv_sem=c_recv.at[part],
            device_id={"scen": flip(scen, 1)},
            device_id_type=MESH,
        )

    def y_copy(index, bit, part):
        return pltpu.make_async_remote_copy(
            src_ref=mine.at[index, part],
            dst_ref=y_in.at[index, part],
            send_sem=y_send.at[index, part],
            recv_sem=y_recv.at[index, part],
            device_id={"scen": flip(scen, bit)},
            device_id_type=MESH,
        )

    for part in range(CHUNKS):
        out_half[part] = term(1 - core, part)
        c_copy(part).start()

    def t_step(index):
        t_copy(index).wait_recv()
        before = t_own[pl.ds(t_mine, t_half), :] if index == 0 else t_sum[index - 1]
        t_sum[index] = before + t_in[index]
        t_copy(index + 1).start()
        if index + 1 == len(scen_bits):
            t_all[pl.ds(t_mine, t_half), :] = t_sum[index]

    t_step(0)
    for part in range(CHUNKS):
        mine[0, part] = term(core, part)
    y_bits = scen_bits[1:]
    for part in range(CHUNKS):
        c_copy(part).wait_recv()
        mine[0, part] += in_half[part]
        y_copy(0, y_bits[0], part).start()
    for index in range(1, len(scen_bits)):
        t_step(index)
    t_copy(len(scen_bits)).wait_recv()
    whole = t_all[...]
    symmetric = 0.5 * (whole + whole.T)
    panels = window // PANEL
    inverses, lowers = [], []

    def matmul_t(lhs, rhs):
        return lax.dot_general(
            lhs, rhs, (((1,), (1,)), ((), ())),
            precision=HIGH, preferred_element_type=F32,
        )

    def next_panel(index):
        low = index * PANEL
        block = symmetric[low:, low:low + PANEL]
        for earlier in range(index):
            rest = lowers[earlier][low - earlier * PANEL:, :]
            block = block - matmul_t(rest, rest[:PANEL, :])
        inverse = panel_inverse(block[:PANEL, :], BLOCK)
        inverses.append(inverse)
        lowers.append(matmul_t(block, inverse))

    next_panel(0)

    def g_copy(part):
        start = pl.multiple_of(core * half + part * chunk, 8)
        return pltpu.make_async_remote_copy(
            src_ref=mine.at[len(y_bits), part],
            dst_ref=h_ref.at[pl.ds(start, chunk), :],
            send_sem=g_send.at[part],
            recv_sem=g_recv.at[part],
            device_id={"scen": flip(scen, 1)},
            device_id_type=MESH,
        )

    def y_step(index, part):
        y_copy(index, y_bits[index], part).wait_recv()
        total_part = mine[index, part] + y_in[index, part]
        start = pl.multiple_of(core * half + part * chunk, 8)
        if index + 1 == len(y_bits):
            total_part = total_part + (
                base[pl.ds(start, chunk), :]
                + onehot[pl.ds(start, chunk), :].astype(F32) * bsel
            )
        mine[index + 1, part] = total_part
        if index + 1 < len(y_bits):
            y_copy(index + 1, y_bits[index + 1], part).start()
        else:
            h_ref[pl.ds(start, chunk), :] = total_part
            g_copy(part).start()

    steps = [(index, part) for index in range(len(y_bits)) for part in range(CHUNKS)]
    early = len(steps) // 2
    for index, part in steps[:early]:
        y_step(index, part)
    for index in range(1, panels):
        next_panel(index)
    for index, part in steps[early:]:
        y_step(index, part)

    m_ref[...] = jnp.zeros_like(m_ref)
    for index in range(panels):
        low = index * PANEL
        for earlier in range(index):
            total = None
            for middle in range(earlier, index):
                across = lowers[middle][low - middle * PANEL:, :][:PANEL, :]
                part = jnp.dot(
                    across,
                    m_ref[middle * PANEL:(middle + 1) * PANEL,
                          earlier * PANEL:(earlier + 1) * PANEL],
                    precision=HIGH, preferred_element_type=F32,
                )
                total = part if total is None else total + part
            m_ref[low:low + PANEL, earlier * PANEL:(earlier + 1) * PANEL] = -jnp.dot(
                inverses[index], total, precision=HIGH, preferred_element_type=F32
            )
        m_ref[low:low + PANEL, low:low + PANEL] = inverses[index]
    for part in range(CHUNKS):
        g_copy(part).wait()

    for one in sent:
        one.wait_send()
    for step in range(1, n_row):
        dst = (row + step) % n_row
        rs_copy(picked.at[dst], parts.at[row], rs_send, rs_recv, dst, dst, row).wait_send()
        rs_copy(fpick.at[dst], fparts.at[row], fs_send, fs_recv, dst, dst, row).wait_send()
    for index in range(len(scen_bits) + 1):
        t_copy(index).wait_send()
    for part in range(CHUNKS):
        c_copy(part).wait_send()
        for index, bit in enumerate(y_bits):
            y_copy(index, bit, part).wait_send()


def per_device(
    n_scen, n_row,
    borders, kkt_inverse, first_section, barrier, panel_vars, probability, assignment,
):
    rows, window = first_section.shape
    depth = kkt_inverse.shape[1]
    full = kkt_inverse.shape[2]
    groups = max(1, min(n_scen, window // (8 * n_row)))
    frow = window // groups // n_row
    stages = n_scen.bit_length() - 1
    half_chunk = rows // 2 // CHUNKS
    dma = pltpu.SemaphoreType.DMA
    vmem = pl.BlockSpec(memory_space=pltpu.VMEM)
    schur, inverse = pl.pallas_call(
        functools.partial(schur_kernel, n_scen, n_row),
        out_shape=(
            jax.ShapeDtypeStruct((rows, window), F32),
            jax.ShapeDtypeStruct((window, window), F32),
        ),
        in_specs=[vmem] * 4 + [pl.BlockSpec(memory_space=pl.ANY)] * 3,
        out_specs=(vmem, vmem),
        scratch_shapes=[
            pltpu.VMEM((full, rows), BF16),
            pltpu.VMEM((depth, full), BF16),
            pltpu.VMEM((rows, window), F32),
            dma((n_row,)), dma((2,)),
            pltpu.VMEM((window, SUB), jnp.int32),
            pltpu.VMEM((rows, window), BF16),
            pltpu.VMEM((n_row, depth, window), BF16),
            pltpu.VMEM((n_row, depth, window), BF16),
            pltpu.VMEM((n_row, depth, window), BF16),
            pltpu.VMEM((n_row, depth, window), BF16),
            pltpu.VMEM((n_row, frow, window), F32),
            pltpu.VMEM((n_row, frow, window), F32),
            pltpu.VMEM((n_row, frow, window), F32),
            pltpu.VMEM((rows, full), BF16),
            pltpu.VMEM((window, window), F32),
            pltpu.VMEM((stages, window // 2, window), F32),
            pltpu.VMEM((stages, window // 2, window), F32),
            pltpu.VMEM((window, window), F32),
            pltpu.VMEM((CHUNKS, half_chunk, window), F32),
            pltpu.VMEM((CHUNKS, half_chunk, window), F32),
            pltpu.VMEM((stages, CHUNKS, half_chunk, window), F32),
            pltpu.VMEM((stages - 1, CHUNKS, half_chunk, window), F32),
            *[dma((n_row,))] * 10,
            dma((stages + 1,)), dma((stages + 1,)),
            dma((CHUNKS,)), dma((CHUNKS,)),
            dma((stages - 1, CHUNKS)), dma((stages - 1, CHUNKS)),
            dma((CHUNKS,)), dma((CHUNKS,)),
        ],
        compiler_params=pltpu.CompilerParams(collective_id=0, has_side_effects=True),
    )(
        panel_vars[None, :], probability[None, :], assignment[:, None],
        barrier, borders[0], kkt_inverse[0], first_section,
    )
    return lax.dot_general(
        schur, inverse, (((1,), (1,)), ((), ())),
        precision=HIGH, preferred_element_type=F32,
    )


def solution(mesh):
    placed = (
        P("scen", None, "row"),
        P("scen", "row", None),
        P("row", None),
        P("row"),
        P(),
        P(),
        P("scen"),
    )
    return jax.shard_map(
        functools.partial(per_device, mesh.shape["scen"], mesh.shape["row"]),
        mesh=mesh, in_specs=placed, out_specs=P("row", None), check_vma=False,
    )
```

profile of v0, /device:TPU:0, one launch (start us, length us, event | category | flops | bytes accessed | tf_op | source)
XLA Modules:
  0.0 74.8 jit_solution(11076956568224279116)
XLA Ops:
  0.7 70.1 %shard_map.73 = (f32[1536,256]{1,0:T(8,128)}, f32[256,256]{1,0:T(8,128)}) custom-call(s32[1,256]{1,0:T(1,128)} %bitcast.10, f32[1,4]{1,0:T(1,128)} %bitcast.11, s32[1,1]{1,0:T(1,128)} %bitcast.7.asg, f32[1536]{0:T(1024)} %bar_row.1, bf16[1024,1536]{1,0:T(8,128)(2,1)} %bitcast.8, bf16[128,1024]{1,0:T(8,128)(2,1)} %bitcast.9, f32[1536,256]{1,0:T(8,128)} %base_hbm.1), custom_call_target="tpu_custom_call" | custom-call | tf_op jit(solution)/shard_map/pallas_call | solution.py:489
  70.8 4.0 %fusion = f32[1536,256]{1,0:T(8,128)} fusion(f32[1536,256]{1,0:T(8,128)} %get-tuple-element.7, f32[256,256]{1,0:T(8,128)} %get-tuple-element.8), kind=kOutput, calls=%fused_computation | convolution fusion | flops 1207959552 | bytes 3407872 | tf_op jit(solution)/shard_map/dot_general | solution.py:531
where the time goes:
time: 75 us; the launch traced here: 74.8 us
  Pallas kernels  70.1 us (93%)
  matrix products  4 us (5%)
    pallas_call x1, Pallas kernels, per_device(): pl.pallas_call(functools.partial(schur_kernel, n_scen, n_row), out_shape=...  70.1 us
    dot_general x1, matrix products, per_device(): lax.dot_general(schur, inverse, (((1,), (1,)), ((), ())), precision=HIGH,...  4 us

commit v1 on v0

v1 whole, which is shorter than its diff:
```python
import functools

import jax
import jax.numpy as jnp
from jax import lax
from jax.experimental import pallas as pl
from jax.experimental.pallas import tpu as pltpu
from jax.sharding import PartitionSpec as P

PANEL = 128
MESH = pl.DeviceIdType.MESH
HIGH = lax.Precision.HIGHEST
F32 = jnp.float32
BF16 = jnp.bfloat16
PARTS = 3
SUB = 8
BLOCK = 32


def small_factor(tile, first):
    shape = tile.shape
    spread = [
        jnp.broadcast_to(tile[:, first + k:first + k + 1], shape) for k in range(SUB)
    ]
    cell = {
        (i, k): jnp.broadcast_to(spread[k][i:i + 1, :], shape)
        for k in range(SUB) for i in range(k, SUB)
    }
    scale, lower = [], {}
    for j in range(SUB):
        scale.append(lax.rsqrt(cell[j, j]))
        for i in range(j + 1, SUB):
            lower[i, j] = cell[i, j] * scale[j]
        for k in range(j + 1, SUB):
            for i in range(k, SUB):
                cell[i, k] = cell[i, k] - lower[i, j] * lower[k, j]
    inverse = {}
    for j in range(SUB):
        inverse[j, j] = scale[j]
        for i in range(j + 1, SUB):
            total = lower[i, j] * inverse[j, j]
            for m in range(j + 1, i):
                total = total + lower[i, m] * inverse[m, j]
            inverse[i, j] = -(scale[i] * total)
    return inverse


def panel_inverse(block, size, hook=None):
    panel = block.shape[0]
    shape = (SUB, panel)
    sub = lax.broadcasted_iota(jnp.int32, shape, 0)
    lane = lax.broadcasted_iota(jnp.int32, shape, 1)
    tiles = panel // SUB
    left = [block[low:low + SUB, :] for low in range(0, panel, SUB)]
    right = [jnp.where(lane == sub + low, 1.0, 0.0) for low in range(0, panel, SUB)]
    per = size // SUB
    for base in range(0, tiles, per):
        for own in range(base, base + per):
            first = own * SUB
            inverse = small_factor(left[own], first)
            new_left = new_right = None
            for k in range(SUB):
                coeff = inverse[SUB - 1, k]
                for i in range(SUB - 2, k - 1, -1):
                    coeff = jnp.where(sub <= i, inverse[i, k], coeff)
                if k:
                    coeff = jnp.where(sub < k, 0.0, coeff)
                add_left = coeff * left[own][k:k + 1, :]
                add_right = coeff * right[own][k:k + 1, :]
                new_left = add_left if k == 0 else new_left + add_left
                new_right = add_right if k == 0 else new_right + add_right
            for tile in range(own + 1, base + per):
                spread = [
                    jnp.broadcast_to(left[tile][:, first + m:first + m + 1], shape)
                    for m in range(SUB)
                ]
                for k in range(SUB):
                    factor = spread[0] * inverse[k, 0]
                    for m in range(1, k + 1):
                        factor = factor + spread[m] * inverse[k, m]
                    left[tile] = left[tile] - factor * new_left[k:k + 1, :]
                    right[tile] = right[tile] - factor * new_right[k:k + 1, :]
            left[own], right[own] = new_left, new_right
        if base + per < tiles:
            upper = jnp.concatenate(left[base:base + per], axis=0)
            both = jnp.concatenate(
                [upper, jnp.concatenate(right[base:base + per], axis=0)], axis=1
            )
            change = lax.dot_general(
                upper, both, (((0,), (0,)), ((), ())),
                precision=HIGH, preferred_element_type=F32,
            )
            for tile in range(base + per, tiles):
                low = tile * SUB
                left[tile] = left[tile] - change[low:low + SUB, :panel]
                right[tile] = right[tile] - change[low:low + SUB, panel:]
        if hook is not None:
            hook(base // per)
    return jnp.concatenate(right, axis=0)


def flip(index, bit):
    return index + bit * (1 - 2 * ((index // bit) % 2))


def toggle(index, mask):
    bit = 1
    while bit <= mask:
        if mask & bit:
            index = flip(index, bit)
        bit *= 2
    return index


def bits_down(count):
    bits = []
    bit = count // 2
    while bit >= 1:
        bits.append(bit)
        bit //= 2
    return bits


def low_bit(mask):
    return mask & -mask


def split3(value):
    high = value.astype(BF16)
    rest = value - high.astype(F32)
    middle = rest.astype(BF16)
    low = (rest - middle.astype(F32)).astype(BF16)
    return high, middle, low


def matmul_t(lhs, rhs):
    return lax.dot_general(
        lhs, rhs, (((1,), (1,)), ((), ())),
        precision=HIGH, preferred_element_type=F32,
    )


def schur_kernel(
    n_scen, n_row,
    pv_row, pv_s, prob, asg, bar_row, b_hbm, k_hbm, base_hbm,
    out_ref,
    b_ref, k_ref, base, load_sem, rest_sem, onehot,
    picked, xin, zsum, zin, columns, solved,
    fpick, fxin, fsum, fzin, fall,
    bt, ct, tf, t_sum, t_in,
    out_half, in_half, mine, y_in, hbuf,
    rsx_send, rsx_recv, rsz_send, rsz_recv,
    cz_send, cz_recv, cx_send, cx_recv,
    sz_send, sz_recv, sx_send, sx_recv,
    t_send, t_recv, c_send, c_recv, y_send, y_recv, g_send, g_recv,
):
    scen = lax.axis_index("scen")
    row = lax.axis_index("row")
    panels = columns.shape[0]
    depth = columns.shape[2]
    full = n_row * depth
    rows, window = base.shape
    nz = n_row // 2
    z, x = row // 2, row % 2
    other = flip(row, 1)
    barrier = pltpu.get_barrier_semaphore()
    scen_bits = bits_down(n_scen)[::-1]
    y_bits = scen_bits[1:]
    near = [toggle(z, step) for step in range(1, nz)]
    far = near[::-1]
    frow = fpick.shape[1]
    frows = n_row * frow
    groups = window // frows
    fstart = (scen % groups) * frows
    first = row * rows
    sent, given = [], {}

    pl.semaphore_signal(barrier, inc=1, device_id={"row": other}, device_id_type=MESH)
    for peer in far:
        pl.semaphore_signal(
            barrier, inc=1, device_id={"row": 2 * peer + x}, device_id_type=MESH
        )
    for bit in scen_bits:
        pl.semaphore_signal(
            barrier, inc=1, device_id={"scen": flip(scen, bit)}, device_id_type=MESH
        )

    def load(block):
        start = pl.multiple_of(block * depth, depth)
        return pltpu.make_async_copy(
            b_hbm.at[pl.ds(start, depth), :],
            b_ref.at[pl.ds(start, depth), :],
            load_sem.at[block],
        )

    base_load = pltpu.make_async_copy(base_hbm, base, rest_sem.at[0])
    k_load = pltpu.make_async_copy(k_hbm, k_ref, rest_sem.at[1])
    for peer in far + [z]:
        load(2 * peer + 1 - x).start()
    for peer in far + [z]:
        load(2 * peer + x).start()
    base_load.start()
    k_load.start()

    onehot[...] = jnp.where(
        lax.broadcasted_iota(jnp.int32, (rows, window), 0) == pv_row[...] - first,
        1.0, 0.0,
    ).astype(BF16)
    bar = split3(bar_row[...].reshape(1, rows))
    level = lax.broadcasted_iota(jnp.int32, (2 * SUB, rows), 0)
    bars = jnp.where(
        level == 0, bar[0].astype(F32),
        jnp.where(level == 1, bar[1].astype(F32),
                  jnp.where(level == 2, bar[2].astype(F32), 0.0)),
    ).astype(BF16)

    pl.semaphore_wait(barrier, nz + len(scen_bits))

    def remote(src, dst, send, recv, where):
        return pltpu.make_async_remote_copy(
            src_ref=src, dst_ref=dst, send_sem=send, recv_sem=recv,
            device_id=where, device_id_type=MESH,
        )

    def go(copy):
        copy.start()
        sent.append(copy)

    pick_of = [picked.at[p] for p in range(panels)] + [fpick]
    xin_of = [xin.at[p] for p in range(panels)] + [fxin]
    zsum_of = [zsum.at[p] for p in range(panels)] + [fsum]
    zin_of = [zin.at[p] for p in range(panels)] + [fzin]
    col_of = [columns.at[p] for p in range(panels)] + [fall]
    sol_of = [solved.at[p] for p in range(panels)]

    def rsx(p, peer):
        return remote(
            pick_of[p].at[2 * peer + 1 - x], xin_of[p].at[peer],
            rsx_send.at[p, peer], rsx_recv.at[p, peer], {"row": other},
        )

    def rsz_go(p, peer):
        go(remote(
            zsum_of[p].at[peer], zin_of[p].at[z],
            rsz_send.at[p, peer], rsz_recv.at[p, z], {"row": 2 * peer + x},
        ))

    def rsz_wait(p, peer):
        remote(
            zsum_of[p].at[peer], zin_of[p].at[peer],
            rsz_send.at[p, peer], rsz_recv.at[p, peer], {"row": 2 * peer + x},
        ).wait_recv()

    def rs_turn(p):
        for peer in far + [z]:
            rsx(p, peer).wait_recv()
            zsum_of[p][peer] = pick_of[p][2 * peer + x] + xin_of[p][peer]
            if peer is not z:
                rsz_go(p, peer)

    def rs_end(p):
        total = zsum_of[p][z].astype(F32)
        for peer in near:
            rsz_wait(p, peer)
            total = total + zin_of[p][peer].astype(F32)
        col_of[p][row] = total.astype(col_of[p].dtype)

    cols = (col_of, cz_send, cz_recv, cx_send, cx_recv)
    sols = (sol_of, sz_send, sz_recv, sx_send, sx_recv)

    def ag_x(kind, p, peer):
        held, _, _, xs, xr = kind
        return remote(
            held[p].at[2 * peer + x], held[p].at[2 * peer + x],
            xs.at[p, peer], xr.at[p, peer], {"row": other},
        )

    def ag_start(kind, p):
        held, zs, zr, _, _ = kind
        for peer in far:
            go(remote(
                held[p].at[row], held[p].at[row],
                zs.at[p, peer], zr.at[p, z], {"row": 2 * peer + x},
            ))
        go(ag_x(kind, p, z))

    def ag_pass(kind, p, peer):
        held, zs, zr, _, _ = kind
        remote(
            held[p].at[2 * peer + x], held[p].at[2 * peer + x],
            zs.at[p, peer], zr.at[p, peer], {"row": 2 * peer + x},
        ).wait_recv()
        go(ag_x(kind, p, peer))

    def ag_end(kind, p):
        held, _, _, xs, xr = kind
        for peer in [z] + near:
            remote(
                held[p].at[2 * peer + 1 - x], held[p].at[2 * peer + 1 - x],
                xs.at[p, peer], xr.at[p, peer], {"row": other},
            ).wait_recv()

    def pick(dst):
        load(dst).wait()
        start = pl.multiple_of(dst * depth, depth)
        block = jnp.dot(
            b_ref[pl.ds(start, depth), :], onehot[...], preferred_element_type=F32
        ).astype(BF16)
        for p in range(panels):
            picked[p, dst] = block[:, p * PANEL:(p + 1) * PANEL]

    for peer in far + [z]:
        pick(2 * peer + 1 - x)
        go(rsx(0, peer))
    for p in range(1, panels):
        for peer in far + [z]:
            go(rsx(p, peer))
    for peer in far + [z]:
        pick(2 * peer + x)

    for p in range(panels):
        rs_turn(p)

    bsel = jnp.sum(
        jnp.dot(bars, onehot[...], preferred_element_type=F32), axis=0, keepdims=True
    )
    base_load.wait()
    slot_row = lax.broadcasted_iota(jnp.int32, (frow, window), 0) + fstart
    slot_col = lax.broadcasted_iota(jnp.int32, (frow, window), 1)

    def frag(block, carry):
        lines = []
        for i in range(frow):
            at = pv_s[fstart + block * frow + i] - first
            inside = jnp.logical_and(at >= 0, at < rows)
            line = base[pl.ds(jnp.clip(at, 0, rows - 1), 1), :]
            lines.append(jnp.where(inside, line, 0.0))
        fpick[block] = jnp.concatenate(lines, axis=0) + jnp.where(
            slot_row + block * frow == slot_col, bsel, 0.0
        )
        return carry

    lax.fori_loop(0, n_row, frag, 0)
    for peer in far + [z]:
        go(rsx(panels, peer))

    def turn(tile, carry):
        start = pl.multiple_of(tile * PANEL, PANEL)
        bt[pl.ds(start, PANEL), :] = b_ref[:, pl.ds(start, PANEL)].T
        return carry

    lax.fori_loop(0, rows // PANEL, turn, 0)

    rs_end(0)
    ag_start(cols, 0)
    base[...] += onehot[...].astype(F32) * bsel
    rs_turn(panels)
    ag_pass(cols, 0, near[0])
    rs_end(1)
    ag_start(cols, 1)
    for peer in near[1:]:
        ag_pass(cols, 0, peer)
    rs_end(panels)
    ag_start(cols, panels)
    k_load.wait()
    ag_pass(cols, 1, near[0])

    def solve(p):
        solved[p, row] = jnp.dot(
            k_ref[...], columns[p].reshape(full, PANEL), preferred_element_type=F32
        ).astype(BF16)

    def side(p):
        ct[p] = columns[p].reshape(full, PANEL).T

    ag_end(cols, 0)
    solve(0)
    ag_start(sols, 0)
    for peer in near[1:]:
        ag_pass(cols, 1, peer)
    side(0)
    ag_pass(sols, 0, near[0])
    for peer in near:
        ag_pass(cols, panels, peer)
    ag_end(cols, 1)
    solve(1)
    ag_start(sols, 1)
    for peer in near[1:]:
        ag_pass(sols, 0, peer)
    side(1)
    ag_end(cols, panels)
    tf[...] = jnp.zeros_like(tf)
    keep = jnp.where(scen < groups, 1.0, 0.0)
    tf[pl.ds(pl.multiple_of(fstart, SUB), frows), :] = fall[...].reshape(frows, window) * keep
    match = lax.broadcasted_iota(jnp.int32, prob.shape, 1) == asg[...]
    weight = jnp.sum(jnp.where(match, prob[...], 0.0), axis=1, keepdims=True)
    for peer in near[:-1]:
        ag_pass(sols, 1, peer)

    def t_block(p, q):
        return weight * jnp.dot(
            ct[p], solved[q].reshape(full, PANEL), preferred_element_type=F32
        ) + tf[p * PANEL:(p + 1) * PANEL, q * PANEL:(q + 1) * PANEL]

    spans = [pl.ds(0, PANEL), pl.ds(PANEL, 2 * PANEL)]

    def t_copy(which, index):
        return remote(
            t_sum.at[index, spans[which]], t_in.at[index, spans[which]],
            t_send.at[which, index], t_recv.at[which, index],
            {"scen": flip(scen, scen_bits[index])},
        )

    def t_step(which, index):
        t_copy(which, index).wait_recv()
        t_sum[index + 1, spans[which]] = (
            t_sum[index, spans[which]] + t_in[index, spans[which]]
        )
        if index + 1 < len(scen_bits):
            go(t_copy(which, index + 1))

    core = scen % 2
    half = rows // 2
    chunk = half // PARTS
    parts = range(PARTS)

    def place(which, part):
        return pl.ds(pl.multiple_of(which * half + part * chunk, SUB), chunk)

    def term(which, p, part):
        return weight * jnp.dot(
            bt[place(which, part), :], solved[p].reshape(full, PANEL),
            preferred_element_type=F32,
        )

    def c_copy(p, part):
        return remote(
            out_half.at[p, part], in_half.at[p, part],
            c_send.at[p, part], c_recv.at[p, part], {"scen": flip(scen, 1)},
        )

    def y_copy(index, p, part):
        return remote(
            mine.at[index, p, part], y_in.at[index, p, part],
            y_send.at[index, p, part], y_recv.at[index, p, part],
            {"scen": flip(scen, y_bits[index])},
        )

    def g_copy(p, part, which):
        return remote(
            hbuf.at[p, place(which, part)], hbuf.at[p, place(which, part)],
            g_send.at[p, part], g_recv.at[p, part], {"scen": flip(scen, 1)},
        )

    def h_out(p):
        for part in parts:
            out_half[p, part] = term(1 - core, p, part)
            go(c_copy(p, part))

    def h_mine(p):
        for part in parts:
            mine[0, p, part] = term(core, p, part)

    def h_join(p, part):
        c_copy(p, part).wait_recv()
        mine[0, p, part] += in_half[p, part]
        go(y_copy(0, p, part))

    def y_step(p, part):
        for index in range(len(y_bits)):
            y_copy(index, p, part).wait_recv()
            total = mine[index, p, part] + y_in[index, p, part]
            if index + 1 < len(y_bits):
                mine[index + 1, p, part] = total
                go(y_copy(index + 1, p, part))
            else:
                hbuf[p, place(core, part)] = (
                    total + base[place(core, part), p * PANEL:(p + 1) * PANEL]
                )
                give = g_copy(p, part, core)
                give.start()
                given[p, part] = give

    ag_end(sols, 0)
    whole = t_block(0, 0)
    t_sum[0, spans[0]] = 0.5 * (whole + whole.T)
    go(t_copy(0, 0))
    for peer in near[-1:]:
        ag_pass(sols, 1, peer)
    h_out(0)
    t_step(0, 0)
    h_mine(0)
    h_join(0, 0)

    ag_end(sols, 1)
    t_sum[0, PANEL:2 * PANEL] = 0.5 * (t_block(1, 0) + t_block(0, 1).T)
    whole = t_block(1, 1)
    t_sum[0, 2 * PANEL:] = 0.5 * (whole + whole.T)
    go(t_copy(1, 0))
    h_out(1)
    t_step(1, 0)
    for part in parts[1:]:
        h_join(0, part)
    for index in range(1, len(scen_bits)):
        t_step(0, index)
    last = len(scen_bits)
    inverse_0 = panel_inverse(t_sum[last, spans[0]], BLOCK)
    for index in range(1, len(scen_bits)):
        t_step(1, index)
    h_mine(1)
    for part in parts:
        h_join(1, part)
    lower = matmul_t(t_sum[last, PANEL:2 * PANEL], inverse_0)
    block = t_sum[last, 2 * PANEL:] - matmul_t(lower, lower)

    def hook(stage):
        if stage < PARTS:
            y_step(0, stage)

    inverse_1 = panel_inverse(block, BLOCK, hook)

    def drop(p, which, part):
        if p == 0:
            left = matmul_t(hbuf[0, place(which, part)], inverse_0)
            out_ref[place(which, part), :PANEL] = left
            hbuf[0, place(which, part)] = matmul_t(left, lower)
        else:
            rest = hbuf[1, place(which, part)] - hbuf[0, place(which, part)]
            out_ref[place(which, part), PANEL:] = matmul_t(rest, inverse_1)

    for part in parts:
        g_copy(0, part, 1 - core).wait_recv()
        drop(0, 1 - core, part)
    for part in parts:
        given.pop((0, part)).wait_send()
        drop(0, core, part)
    for part in parts:
        y_step(1, part)
        drop(1, core, part)
    for part in parts:
        g_copy(1, part, 1 - core).wait_recv()
        drop(1, 1 - core, part)
    for one in sent + list(given.values()):
        one.wait_send()


def per_device(
    n_scen, n_row,
    borders, kkt_inverse, first_section, barrier, panel_vars, probability, assignment,
):
    rows, window = first_section.shape
    depth = kkt_inverse.shape[1]
    full = kkt_inverse.shape[2]
    panels = window // PANEL
    nz = n_row // 2
    groups = max(1, min(n_scen, window // (8 * n_row)))
    frow = window // groups // n_row
    stages = n_scen.bit_length() - 1
    chunk = rows // 2 // PARTS
    dma = pltpu.SemaphoreType.DMA
    vmem = pl.BlockSpec(memory_space=pltpu.VMEM)
    smem = pl.BlockSpec(memory_space=pltpu.SMEM)

    def buf(shape, dtype):
        return pltpu.VMEM(shape, dtype)

    return pl.pallas_call(
        functools.partial(schur_kernel, n_scen, n_row),
        out_shape=jax.ShapeDtypeStruct((rows, window), F32),
        in_specs=[vmem, smem] + [vmem] * 3 + [pl.BlockSpec(memory_space=pl.ANY)] * 3,
        out_specs=vmem,
        scratch_shapes=[
            buf((full, rows), BF16), buf((depth, full), BF16), buf((rows, window), F32),
            dma((n_row,)), dma((2,)), buf((rows, window), BF16),
            buf((panels, n_row, depth, PANEL), BF16),
            buf((panels, nz, depth, PANEL), BF16),
            buf((panels, nz, depth, PANEL), BF16),
            buf((panels, nz, depth, PANEL), BF16),
            buf((panels, n_row, depth, PANEL), BF16),
            buf((panels, n_row, depth, PANEL), BF16),
            buf((n_row, frow, window), F32),
            buf((nz, frow, window), F32),
            buf((nz, frow, window), F32),
            buf((nz, frow, window), F32),
            buf((n_row, frow, window), F32),
            buf((rows, full), BF16), buf((panels, PANEL, full), BF16),
            buf((window, window), F32),
            buf((stages + 1, 3 * PANEL, PANEL), F32),
            buf((stages, 3 * PANEL, PANEL), F32),
            buf((panels, PARTS, chunk, PANEL), F32),
            buf((panels, PARTS, chunk, PANEL), F32),
            buf((stages - 1, panels, PARTS, chunk, PANEL), F32),
            buf((stages - 1, panels, PARTS, chunk, PANEL), F32),
            buf((panels, rows, PANEL), F32),
            *[dma((panels + 1, nz))] * 8,
            *[dma((panels, nz))] * 4,
            *[dma((2, stages))] * 2,
            *[dma((panels, PARTS))] * 2,
            *[dma((stages - 1, panels, PARTS))] * 2,
            *[dma((panels, PARTS))] * 2,
        ],
        compiler_params=pltpu.CompilerParams(collective_id=0, has_side_effects=True),
    )(
        panel_vars[None, :], panel_vars, probability[None, :], assignment[:, None],
        barrier, borders[0], kkt_inverse[0], first_section,
    )


def solution(mesh):
    placed = (
        P("scen", None, "row"),
        P("scen", "row", None),
        P("row", None),
        P("row"),
        P(),
        P(),
        P("scen"),
    )
    return jax.shard_map(
        functools.partial(per_device, mesh.shape["scen"], mesh.shape["row"]),
        mesh=mesh, in_specs=placed, out_specs=P("row", None), check_vma=False,
    )
```

time: 75 us -> 66.8 us (0.89)
  Pallas kernels: 70.1 us -> 63.3 us
  matrix products: 4 us -> 0 us
  local copies, waits for them, and re-layouts: 0 us -> 2.65 us
    pallas_call x1, Pallas kernels: 70.1 us -> 63.3 us  [per_device(): pl.pallas_call(functools.partial(schur_kernel, n_scen, n_row), out_shape=...]
    dot_general x1 -> x0, matrix products: 4 us -> none  [per_device(): lax.dot_general(schur, inverse, (((1,), (1,)), ((), ())), precision=HIGH,...]
    unnamed x0 -> x1, local copies, waits for them, and re-layouts: none -> 2.65 us
where the time goes in v1:
time: 66.8 us; the launch traced here: 66.6 us
  Pallas kernels  63.3 us (95%)
  local copies, waits for them, and re-layouts  2.65 us (4%)
    pallas_call x1, Pallas kernels, per_device(): pl.pallas_call(functools.partial(schur_kernel, n_scen, n_row), out_shape=...  63.3 us
    unnamed x1, local copies, waits for them, and re-layouts  2.65 us

profile of v1, /device:TPU:0, one launch (start us, length us, event | category | flops | bytes accessed | tf_op | source)
XLA Modules:
  0.0 66.6 jit_solution(4984929671252932784)
XLA Ops:
  0.7 63.3 %shard_map.73 = f32[1536,256]{1,0:T(8,128)} custom-call(s32[1,256]{1,0:T(1,128)} %bitcast.8, s32[256]{0:T(256)} %pv_s.1, f32[1,4]{1,0:T(1,128)} %bitcast.9, s32[1,1]{1,0:T(1,128)} %bitcast.5.asg, f32[1536]{0:T(1024)} %bar_row.1, bf16[1024,1536]{1,0:T(8,128)(2,1)} %bitcast.6, bf16[128,1024]{1,0:T(8,128)(2,1)} %bitcast.7, f32[1536,256]{1,0:T(8,128)} %base_hbm.1), custom_call_target="tpu_custom_call" | custom-call | tf_op jit(solution)/shard_map/pallas_call | solution.py:567
  64.0 2.7 %copy.10 = f32[1536,256]{1,0:T(8,128)} copy(f32[1536,256]{1,0:T(8,128)} %shard_map.73) | data formatting | bytes 3145728

commit v2 on v1

--- a/solution.py
+++ b/solution.py
@@ -15,6 +15,10 @@
 PARTS = 3
 SUB = 8
 BLOCK = 32
+MAIN_VMEM = 40 << 20
+LAST_VMEM = 8 << 20
+STEPS = 32766.0
+TINY = 1e-30
 
 
 def small_factor(tile, first):
@@ -43,6 +47,11 @@
                 total = total + lower[i, m] * inverse[m, j]
             inverse[i, j] = -(scale[i] * total)
     return inverse
+
+
+def split2(value):
+    high = value.astype(BF16)
+    return high, (value - high.astype(F32)).astype(BF16)
 
 
 def panel_inverse(block, size, hook=None):
@@ -86,9 +95,13 @@
             both = jnp.concatenate(
                 [upper, jnp.concatenate(right[base:base + per], axis=0)], axis=1
             )
+            high, low = split2(both)
             change = lax.dot_general(
-                upper, both, (((0,), (0,)), ((), ())),
-                precision=HIGH, preferred_element_type=F32,
+                jnp.concatenate(
+                    [high[:, :panel], high[:, :panel], low[:, :panel]], axis=0
+                ),
+                jnp.concatenate([high, low, high], axis=0),
+                (((0,), (0,)), ((), ())), preferred_element_type=F32,
             )
             for tile in range(base + per, tiles):
                 low = tile * SUB
@@ -133,25 +146,64 @@
     return high, middle, low
 
 
-def matmul_t(lhs, rhs):
-    return lax.dot_general(
-        lhs, rhs, (((1,), (1,)), ((), ())),
-        precision=HIGH, preferred_element_type=F32,
+def wide(*mats):
+    blocks = []
+    for mat in mats:
+        high, low = split2(mat)
+        blocks.append(jnp.concatenate(
+            [jnp.concatenate([high, low], axis=0),
+             jnp.concatenate([high, jnp.zeros_like(low)], axis=0)], axis=1))
+    return jnp.concatenate(blocks, axis=0)
+
+
+def product_t(lhs, stacked):
+    high, low = split2(lhs)
+    both = lax.dot_general(
+        jnp.concatenate([high, low], axis=1), stacked, (((1,), (1,)), ((), ())),
+        preferred_element_type=F32,
     )
+    side = lhs.shape[1]
+    return [
+        both[:, at:at + side] + both[:, at + side:at + 2 * side]
+        for at in range(0, both.shape[1], 2 * side)
+    ]
+
+
+def product(lhs, rhs):
+    high, low = split2(lhs)
+    top, bottom = split2(rhs)
+    both = jnp.dot(
+        jnp.concatenate([high, low], axis=1),
+        jnp.concatenate(
+            [jnp.concatenate([top, bottom], axis=1),
+             jnp.concatenate([top, jnp.zeros_like(top)], axis=1)], axis=0),
+        preferred_element_type=F32,
+    )
+    side = rhs.shape[1]
+    return both[:, :side] + both[:, side:]
+
+
+def code(value):
+    top = jnp.max(jnp.abs(value), axis=0, keepdims=True)
+    unit = jnp.maximum(top, TINY) * (1.0 / STEPS)
+    return jnp.round(value * (1.0 / unit)).astype(jnp.int32).astype(jnp.int16), unit
+
+
+def decode(steps, unit):
+    return steps.astype(jnp.int32).astype(F32) * unit
 
 
 def schur_kernel(
     n_scen, n_row,
-    pv_row, pv_s, prob, asg, bar_row, b_hbm, k_hbm, base_hbm,
-    out_ref,
-    b_ref, k_ref, base, load_sem, rest_sem, onehot,
+    asg, pv_hbm, prob_hbm, bar_hbm, b_hbm, k_hbm, base_hbm,
+    left_ref, right_ref, h_ref, stack_ref,
+    b_ref, k_ref, base, load_sem, rest_sem, pv_row, pv_s, prob, bar_row, onehot,
     picked, xin, zsum, zin, columns, solved,
     fpick, fxin, fsum, fzin, fall,
     bt, ct, tf, t_sum, t_in,
-    out_half, in_half, mine, y_in, hbuf,
-    rsx_send, rsx_recv, rsz_send, rsz_recv,
-    cz_send, cz_recv, cx_send, cx_recv,
-    sz_send, sz_recv, sx_send, sx_recv,
+    first_stack, out_half, in_half, steps, units, steps_in, units_in, h_first,
+    rsx_send, rsz_send, ca_send, sa_send, rsz_recv, cx_recv, sx_recv,
+    rsx_recv, cz_recv, sz_recv,
     t_send, t_recv, c_send, c_recv, y_send, y_recv, g_send, g_recv,
 ):
     scen = lax.axis_index("scen")
@@ -173,7 +225,7 @@
     groups = window // frows
     fstart = (scen % groups) * frows
     first = row * rows
-    sent, given = [], {}
+    done = (h_first, h_ref)
 
     pl.semaphore_signal(barrier, inc=1, device_id={"row": other}, device_id_type=MESH)
     for peer in far:
@@ -195,25 +247,28 @@
 
     base_load = pltpu.make_async_copy(base_hbm, base, rest_sem.at[0])
     k_load = pltpu.make_async_copy(k_hbm, k_ref, rest_sem.at[1])
+    small = [
+        pltpu.make_async_copy(source, to, rest_sem.at[2 + index])
+        for index, (source, to) in enumerate((
+            (pv_hbm, pv_row), (bar_hbm, bar_row), (pv_hbm.at[0], pv_s),
+            (prob_hbm, prob),
+        ))
+    ]
+    small[0].start()
     for peer in far + [z]:
         load(2 * peer + 1 - x).start()
+    for one in small[1:]:
+        one.start()
+    base_load.start()
     for peer in far + [z]:
         load(2 * peer + x).start()
-    base_load.start()
     k_load.start()
 
+    small[0].wait()
     onehot[...] = jnp.where(
         lax.broadcasted_iota(jnp.int32, (rows, window), 0) == pv_row[...] - first,
         1.0, 0.0,
     ).astype(BF16)
-    bar = split3(bar_row[...].reshape(1, rows))
-    level = lax.broadcasted_iota(jnp.int32, (2 * SUB, rows), 0)
-    bars = jnp.where(
-        level == 0, bar[0].astype(F32),
-        jnp.where(level == 1, bar[1].astype(F32),
-                  jnp.where(level == 2, bar[2].astype(F32), 0.0)),
-    ).astype(BF16)
-
     pl.semaphore_wait(barrier, nz + len(scen_bits))
 
     def remote(src, dst, send, recv, where):
@@ -224,7 +279,9 @@
 
     def go(copy):
         copy.start()
-        sent.append(copy)
+
+    def drained(held, sem):
+        remote(held, held, sem, sem, {"row": other}).wait_send()
 
     pick_of = [picked.at[p] for p in range(panels)] + [fpick]
     xin_of = [xin.at[p] for p in range(panels)] + [fxin]
@@ -236,20 +293,18 @@
     def rsx(p, peer):
         return remote(
             pick_of[p].at[2 * peer + 1 - x], xin_of[p].at[peer],
-            rsx_send.at[p, peer], rsx_recv.at[p, peer], {"row": other},
+            rsx_send.at[p], rsx_recv.at[p, peer], {"row": other},
         )
 
     def rsz_go(p, peer):
         go(remote(
             zsum_of[p].at[peer], zin_of[p].at[z],
-            rsz_send.at[p, peer], rsz_recv.at[p, z], {"row": 2 * peer + x},
+            rsz_send.at[p], rsz_recv.at[p], {"row": 2 * peer + x},
         ))
 
-    def rsz_wait(p, peer):
-        remote(
-            zsum_of[p].at[peer], zin_of[p].at[peer],
-            rsz_send.at[p, peer], rsz_recv.at[p, peer], {"row": 2 * peer + x},
-        ).wait_recv()
+    def rsz_wait(p):
+        held = zin_of[p].at[pl.ds(0, nz - 1)]
+        remote(held, held, rsz_send.at[p], rsz_recv.at[p], {"row": other}).wait_recv()
 
     def rs_turn(p):
         for peer in far + [z]:
@@ -260,45 +315,42 @@
 
     def rs_end(p):
         total = zsum_of[p][z].astype(F32)
+        rsz_wait(p)
         for peer in near:
-            rsz_wait(p, peer)
             total = total + zin_of[p][peer].astype(F32)
         col_of[p][row] = total.astype(col_of[p].dtype)
 
-    cols = (col_of, cz_send, cz_recv, cx_send, cx_recv)
-    sols = (sol_of, sz_send, sz_recv, sx_send, sx_recv)
+    cols = (col_of, ca_send, cz_recv, cx_recv)
+    sols = (sol_of, sa_send, sz_recv, sx_recv)
 
     def ag_x(kind, p, peer):
-        held, _, _, xs, xr = kind
+        held, send, _, xr = kind
         return remote(
             held[p].at[2 * peer + x], held[p].at[2 * peer + x],
-            xs.at[p, peer], xr.at[p, peer], {"row": other},
+            send.at[p], xr.at[p], {"row": other},
         )
 
     def ag_start(kind, p):
-        held, zs, zr, _, _ = kind
+        held, send, zr, _ = kind
         for peer in far:
             go(remote(
                 held[p].at[row], held[p].at[row],
-                zs.at[p, peer], zr.at[p, z], {"row": 2 * peer + x},
+                send.at[p], zr.at[p, z], {"row": 2 * peer + x},
             ))
         go(ag_x(kind, p, z))
 
     def ag_pass(kind, p, peer):
-        held, zs, zr, _, _ = kind
+        held, send, zr, _ = kind
         remote(
             held[p].at[2 * peer + x], held[p].at[2 * peer + x],
-            zs.at[p, peer], zr.at[p, peer], {"row": 2 * peer + x},
+            send.at[p], zr.at[p, peer], {"row": 2 * peer + x},
         ).wait_recv()
         go(ag_x(kind, p, peer))
 
     def ag_end(kind, p):
-        held, _, _, xs, xr = kind
-        for peer in [z] + near:
-            remote(
-                held[p].at[2 * peer + 1 - x], held[p].at[2 * peer + 1 - x],
-                xs.at[p, peer], xr.at[p, peer], {"row": other},
-            ).wait_recv()
+        held, send, _, xr = kind
+        some = held[p].at[pl.ds(0, nz)]
+        remote(some, some, send.at[p], xr.at[p], {"row": other}).wait_recv()
 
     def pick(dst):
         load(dst).wait()
@@ -315,11 +367,15 @@
     for p in range(1, panels):
         for peer in far + [z]:
             go(rsx(p, peer))
-    for peer in far + [z]:
-        pick(2 * peer + x)
-
-    for p in range(panels):
-        rs_turn(p)
+    for one in small[1:]:
+        one.wait()
+    bar = split3(bar_row[...].reshape(1, rows))
+    level = lax.broadcasted_iota(jnp.int32, (2 * SUB, rows), 0)
+    bars = jnp.where(
+        level == 0, bar[0].astype(F32),
+        jnp.where(level == 1, bar[1].astype(F32),
+                  jnp.where(level == 2, bar[2].astype(F32), 0.0)),
+    ).astype(BF16)
 
     bsel = jnp.sum(
         jnp.dot(bars, onehot[...], preferred_element_type=F32), axis=0, keepdims=True
@@ -344,27 +400,17 @@
     for peer in far + [z]:
         go(rsx(panels, peer))
 
+    for peer in far + [z]:
+        pick(2 * peer + x)
+
+    for p in range(panels):
+        rs_turn(p)
+
     def turn(tile, carry):
         start = pl.multiple_of(tile * PANEL, PANEL)
         bt[pl.ds(start, PANEL), :] = b_ref[:, pl.ds(start, PANEL)].T
         return carry
 
-    lax.fori_loop(0, rows // PANEL, turn, 0)
-
-    rs_end(0)
-    ag_start(cols, 0)
-    base[...] += onehot[...].astype(F32) * bsel
-    rs_turn(panels)
-    ag_pass(cols, 0, near[0])
-    rs_end(1)
-    ag_start(cols, 1)
-    for peer in near[1:]:
-        ag_pass(cols, 0, peer)
-    rs_end(panels)
-    ag_start(cols, panels)
-    k_load.wait()
-    ag_pass(cols, 1, near[0])
-
     def solve(p):
         solved[p, row] = jnp.dot(
             k_ref[...], columns[p].reshape(full, PANEL), preferred_element_type=F32
@@ -373,29 +419,44 @@
     def side(p):
         ct[p] = columns[p].reshape(full, PANEL).T
 
+    rs_end(0)
+    ag_start(cols, 0)
+    base[...] += onehot[...].astype(F32) * bsel
+    tiles = rows // PANEL
+    lax.fori_loop(0, tiles // 2, turn, 0)
+    ag_pass(cols, 0, near[0])
+    rs_end(1)
+    ag_start(cols, 1)
+    rs_turn(panels)
+    for peer in near[1:]:
+        ag_pass(cols, 0, peer)
+    ag_pass(cols, 1, near[0])
+    lax.fori_loop(tiles // 2, tiles, turn, 0)
+    k_load.wait()
     ag_end(cols, 0)
     solve(0)
     ag_start(sols, 0)
+    rs_end(panels)
+    ag_start(cols, panels)
     for peer in near[1:]:
         ag_pass(cols, 1, peer)
     side(0)
     ag_pass(sols, 0, near[0])
-    for peer in near:
-        ag_pass(cols, panels, peer)
     ag_end(cols, 1)
     solve(1)
     ag_start(sols, 1)
+    for peer in near:
+        ag_pass(cols, panels, peer)
     for peer in near[1:]:
         ag_pass(sols, 0, peer)
     side(1)
+    for peer in near[:-1]:
+        ag_pass(sols, 1, peer)
     ag_end(cols, panels)
     tf[...] = jnp.zeros_like(tf)
     keep = jnp.where(scen < groups, 1.0, 0.0)
     tf[pl.ds(pl.multiple_of(fstart, SUB), frows), :] = fall[...].reshape(frows, window) * keep
-    match = lax.broadcasted_iota(jnp.int32, prob.shape, 1) == asg[...]
-    weight = jnp.sum(jnp.where(match, prob[...], 0.0), axis=1, keepdims=True)
-    for peer in near[:-1]:
-        ag_pass(sols, 1, peer)
+    weight = prob[asg[0]]
 
     def t_block(p, q):
         return weight * jnp.dot(
@@ -436,20 +497,32 @@
     def c_copy(p, part):
         return remote(
             out_half.at[p, part], in_half.at[p, part],
-            c_send.at[p, part], c_recv.at[p, part], {"scen": flip(scen, 1)},
-        )
-
-    def y_copy(index, p, part):
-        return remote(
-            mine.at[index, p, part], y_in.at[index, p, part],
-            y_send.at[index, p, part], y_recv.at[index, p, part],
-            {"scen": flip(scen, y_bits[index])},
-        )
+            c_send.at[0], c_recv.at[p, part], {"scen": flip(scen, 1)},
+        )
+
+    def y_copies(index, p, part):
+        where = {"scen": flip(scen, y_bits[index])}
+        return (
+            remote(
+                steps.at[index, p, part], steps_in.at[index, p, part],
+                y_send.at[0], y_recv.at[0, index, p, part], where,
+            ),
+            remote(
+                units.at[index, p, part], units_in.at[index, p, part],
+                y_send.at[1], y_recv.at[1, index, p, part], where,
+            ),
+        )
+
+    def y_start(index, p, part, value):
+        steps[index, p, part], unit = code(value)
+        units[index, p, part] = jnp.broadcast_to(unit, units.shape[3:])
+        for one in y_copies(index, p, part):
+            go(one)
 
     def g_copy(p, part, which):
         return remote(
-            hbuf.at[p, place(which, part)], hbuf.at[p, place(which, part)],
-            g_send.at[p, part], g_recv.at[p, part], {"scen": flip(scen, 1)},
+            done[p].at[place(which, part), :], done[p].at[place(which, part), :],
+            g_send.at[p], g_recv.at[p], {"scen": flip(scen, 1)},
         )
 
     def h_out(p):
@@ -457,29 +530,25 @@
             out_half[p, part] = term(1 - core, p, part)
             go(c_copy(p, part))
 
-    def h_mine(p):
-        for part in parts:
-            mine[0, p, part] = term(core, p, part)
-
     def h_join(p, part):
+        own = term(core, p, part)
         c_copy(p, part).wait_recv()
-        mine[0, p, part] += in_half[p, part]
-        go(y_copy(0, p, part))
+        y_start(0, p, part, own + in_half[p, part])
 
     def y_step(p, part):
         for index in range(len(y_bits)):
-            y_copy(index, p, part).wait_recv()
-            total = mine[index, p, part] + y_in[index, p, part]
+            for one in y_copies(index, p, part):
+                one.wait_recv()
+            total = decode(
+                steps[index, p, part], units[index, p, part][0:1, :]
+            ) + decode(steps_in[index, p, part], units_in[index, p, part][0:1, :])
             if index + 1 < len(y_bits):
-                mine[index + 1, p, part] = total
-                go(y_copy(index + 1, p, part))
+                y_start(index + 1, p, part, total)
             else:
-                hbuf[p, place(core, part)] = (
+                done[p][place(core, part), :] = (
                     total + base[place(core, part), p * PANEL:(p + 1) * PANEL]
                 )
-                give = g_copy(p, part, core)
-                give.start()
-                given[p, part] = give
+                go(g_copy(p, part, core))
 
     ag_end(sols, 0)
     whole = t_block(0, 0)
@@ -487,61 +556,97 @@
     go(t_copy(0, 0))
     for peer in near[-1:]:
         ag_pass(sols, 1, peer)
+    t_step(0, 0)
     h_out(0)
-    t_step(0, 0)
-    h_mine(0)
     h_join(0, 0)
-
     ag_end(sols, 1)
     t_sum[0, PANEL:2 * PANEL] = 0.5 * (t_block(1, 0) + t_block(0, 1).T)
     whole = t_block(1, 1)
     t_sum[0, 2 * PANEL:] = 0.5 * (whole + whole.T)
     go(t_copy(1, 0))
-    h_out(1)
-    t_step(1, 0)
-    for part in parts[1:]:
-        h_join(0, part)
     for index in range(1, len(scen_bits)):
         t_step(0, index)
     last = len(scen_bits)
-    inverse_0 = panel_inverse(t_sum[last, spans[0]], BLOCK)
+
+    def hook_0(stage):
+        if stage == 0:
+            t_step(1, 0)
+            for part in parts[1:]:
+                h_join(0, part)
+        elif stage == 1:
+            h_out(1)
+        elif stage == 2:
+            for part in parts:
+                h_join(1, part)
+
+    inverse_0 = panel_inverse(t_sum[last, spans[0]], BLOCK, hook_0)
     for index in range(1, len(scen_bits)):
         t_step(1, index)
-    h_mine(1)
-    for part in parts:
-        h_join(1, part)
-    lower = matmul_t(t_sum[last, PANEL:2 * PANEL], inverse_0)
-    block = t_sum[last, 2 * PANEL:] - matmul_t(lower, lower)
+    lower = product_t(t_sum[last, PANEL:2 * PANEL], wide(inverse_0))[0]
+    block = t_sum[last, 2 * PANEL:] - product_t(lower, wide(lower))[0]
+
+    def g_end(p):
+        some = done[p].at[pl.ds(0, half), :]
+        remote(
+            some, some, g_send.at[p], g_recv.at[p], {"scen": flip(scen, 1)}
+        ).wait_recv()
+
+    def drop(which, part):
+        left, right = product_t(h_first[place(which, part), :], first_stack[...])
+        left_ref[place(which, part), :] = left
+        right_ref[place(which, part), :] = right
 
     def hook(stage):
-        if stage < PARTS:
-            y_step(0, stage)
-
-    inverse_1 = panel_inverse(block, BLOCK, hook)
-
-    def drop(p, which, part):
-        if p == 0:
-            left = matmul_t(hbuf[0, place(which, part)], inverse_0)
-            out_ref[place(which, part), :PANEL] = left
-            hbuf[0, place(which, part)] = matmul_t(left, lower)
-        else:
-            rest = hbuf[1, place(which, part)] - hbuf[0, place(which, part)]
-            out_ref[place(which, part), PANEL:] = matmul_t(rest, inverse_1)
-
-    for part in parts:
-        g_copy(0, part, 1 - core).wait_recv()
-        drop(0, 1 - core, part)
-    for part in parts:
-        given.pop((0, part)).wait_send()
-        drop(0, core, part)
-    for part in parts:
-        y_step(1, part)
-        drop(1, core, part)
-    for part in parts:
-        g_copy(1, part, 1 - core).wait_recv()
-        drop(1, 1 - core, part)
-    for one in sent + list(given.values()):
-        one.wait_send()
+        if stage == 0:
+            first_stack[...] = wide(inverse_0, product(lower, inverse_0))
+            for part in parts:
+                y_step(0, part)
+        elif stage == 1:
+            g_end(0)
+            for part in parts:
+                drop(core, part)
+        elif stage == 2:
+            for part in parts:
+                y_step(1, part)
+            for part in parts:
+                drop(1 - core, part)
+
+    stack_ref[...] = wide(panel_inverse(block, BLOCK, hook))
+    g_end(1)
+    for p in range(panels + 1):
+        drained(xin_of[p], rsx_send.at[p])
+        drained(zin_of[p].at[pl.ds(0, nz - 1)], rsz_send.at[p])
+        drained(col_of[p].at[pl.ds(0, n_row - 1)], ca_send.at[p])
+    for p in range(panels):
+        drained(sol_of[p].at[pl.ds(0, n_row - 1)], sa_send.at[p])
+        drained(done[p].at[pl.ds(0, half), :], g_send.at[p])
+    for which in range(2):
+        for index in range(len(scen_bits)):
+            t_copy(which, index).wait_send()
+    drained(out_half, c_send.at[0])
+    drained(steps, y_send.at[0])
+    drained(units, y_send.at[1])
+
+
+def last_kernel(pieces, left_ref, right_ref, h_ref, stack_ref, out_hbm, out, sem):
+    size = out.shape[0] // pieces
+
+    def store(side, piece, source):
+        return pltpu.make_async_copy(
+            source.at[pl.ds(piece * size, size), :],
+            out_hbm.at[pl.ds(piece * size, size), pl.ds(side * PANEL, PANEL)],
+            sem.at[side, piece],
+        )
+
+    for piece in range(pieces):
+        store(0, piece, left_ref).start()
+    for piece in range(pieces):
+        span = pl.ds(piece * size, size)
+        out[span, :] = product_t(h_ref[span, :] - right_ref[span, :], stack_ref[...])[0]
+        store(1, piece, out).start()
+    for piece in range(pieces):
+        store(0, piece, left_ref).wait()
+        store(1, piece, out).wait()
 
 
 def per_device(
@@ -559,19 +664,25 @@
     chunk = rows // 2 // PARTS
     dma = pltpu.SemaphoreType.DMA
     vmem = pl.BlockSpec(memory_space=pltpu.VMEM)
-    smem = pl.BlockSpec(memory_space=pltpu.SMEM)
 
     def buf(shape, dtype):
         return pltpu.VMEM(shape, dtype)
 
-    return pl.pallas_call(
+    held = pl.pallas_call(
         functools.partial(schur_kernel, n_scen, n_row),
-        out_shape=jax.ShapeDtypeStruct((rows, window), F32),
-        in_specs=[vmem, smem] + [vmem] * 3 + [pl.BlockSpec(memory_space=pl.ANY)] * 3,
-        out_specs=vmem,
+        out_shape=(
+            buf((rows, PANEL), F32), buf((rows, PANEL), F32), buf((rows, PANEL), F32),
+            buf((2 * PANEL, 2 * PANEL), BF16),
+        ),
+        in_specs=[pl.BlockSpec(memory_space=pltpu.SMEM)]
+        + [pl.BlockSpec(memory_space=pltpu.HBM)] * 6,
+        out_specs=(vmem,) * 4,
         scratch_shapes=[
             buf((full, rows), BF16), buf((depth, full), BF16), buf((rows, window), F32),
-            dma((n_row,)), dma((2,)), buf((rows, window), BF16),
+            dma((n_row,)), dma((6,)),
+            buf((1, window), jnp.int32), pltpu.SMEM((window,), jnp.int32),
+            pltpu.SMEM((n_scen,), F32), buf((rows,), F32),
+            buf((rows, window), BF16),
             buf((panels, n_row, depth, PANEL), BF16),
             buf((panels, nz, depth, PANEL), BF16),
             buf((panels, nz, depth, PANEL), BF16),
@@ -587,23 +698,37 @@
             buf((window, window), F32),
             buf((stages + 1, 3 * PANEL, PANEL), F32),
             buf((stages, 3 * PANEL, PANEL), F32),
+            buf((4 * PANEL, 2 * PANEL), BF16),
             buf((panels, PARTS, chunk, PANEL), F32),
             buf((panels, PARTS, chunk, PANEL), F32),
-            buf((stages - 1, panels, PARTS, chunk, PANEL), F32),
-            buf((stages - 1, panels, PARTS, chunk, PANEL), F32),
-            buf((panels, rows, PANEL), F32),
-            *[dma((panels + 1, nz))] * 8,
-            *[dma((panels, nz))] * 4,
+            *[buf((stages - 1, panels, PARTS, chunk, PANEL), jnp.int16),
+              buf((stages - 1, panels, PARTS, SUB, PANEL), F32)] * 2,
+            buf((rows, PANEL), F32),
+            *[dma((panels + 1,))] * 3, dma((panels,)), *[dma((panels + 1,))] * 2,
+            dma((panels,)), *[dma((panels + 1, nz))] * 2, dma((panels, nz)),
             *[dma((2, stages))] * 2,
-            *[dma((panels, PARTS))] * 2,
-            *[dma((stages - 1, panels, PARTS))] * 2,
-            *[dma((panels, PARTS))] * 2,
+            dma((1,)), dma((panels, PARTS)),
+            dma((2,)), dma((2, stages - 1, panels, PARTS)),
+            *[dma((panels,))] * 2,
         ],
-        compiler_params=pltpu.CompilerParams(collective_id=0, has_side_effects=True),
+        compiler_params=pltpu.CompilerParams(
+            collective_id=0, has_side_effects=True, vmem_limit_bytes=MAIN_VMEM
+        ),
     )(
-        panel_vars[None, :], panel_vars, probability[None, :], assignment[:, None],
-        barrier, borders[0], kkt_inverse[0], first_section,
+        assignment,
+        *[pltpu.with_memory_space_constraint(one, pltpu.HBM)
+          for one in (panel_vars[None, :], probability, barrier,
+                      borders[0], kkt_inverse[0], first_section)],
     )
+    pieces = 2 * PARTS
+    return pl.pallas_call(
+        functools.partial(last_kernel, pieces),
+        out_shape=jax.ShapeDtypeStruct((rows, window), F32),
+        in_specs=[vmem] * 4,
+        out_specs=pl.BlockSpec(memory_space=pl.ANY),
+        scratch_shapes=[buf((rows, PANEL), F32), dma((2, pieces))],
+        compiler_params=pltpu.CompilerParams(vmem_limit_bytes=LAST_VMEM),
+    )(*[pltpu.with_memory_space_constraint(one, pltpu.VMEM) for one in held])
 
 
 def solution(mesh):

time: 66.8 us -> 55.3 us (0.83)
  Pallas kernels: 63.3 us -> 54.5 us
  local copies, waits for them, and re-layouts: 2.65 us -> 0 us
    pallas_call x1, Pallas kernels: 63.3 us -> 53.2 us  [per_device(): pl.pallas_call(functools.partial(schur_kernel, n_scen, n_row), out_shape=...]
    unnamed x1 -> x0, local copies, waits for them, and re-layouts: 2.65 us -> none
    pallas_call x0 -> x1, Pallas kernels: none -> 1.26 us  [per_device(): pl.pallas_call(functools.partial(last_kernel, pieces), out_shape=jax.Shap...]
where the time goes in v2:
time: 55.3 us; the launch traced here: 55.1 us
  Pallas kernels  54.5 us (99%)
  between operations  0.66 us (1%)
    pallas_call x1, Pallas kernels, per_device(): pl.pallas_call(functools.partial(schur_kernel, n_scen, n_row), out_shape=...  53.2 us
    pallas_call x1, Pallas kernels, per_device(): pl.pallas_call(functools.partial(last_kernel, pieces), out_shape=jax.Shap...  1.26 us

profile of v2, /device:TPU:0, one launch (start us, length us, event | category | flops | bytes accessed | tf_op | source)
XLA Modules:
  0.0 55.1 jit_solution(4600190777348421597)
XLA Ops:
  0.7 53.2 %shard_map.73 = (f32[1536,128]{1,0:T(8,128)S(1)}, f32[1536,128]{1,0:T(8,128)S(1)}, f32[1536,128]{1,0:T(8,128)S(1)}, bf16[256,256]{1,0:T(8,128)(2,1)S(1)}) custom-call(s32[1]{0:T(128)S(6)} %copy.8.asg, s32[1,256]{1,0:T(1,128)} %bitcast.5, f32[4]{0:T(128)} %prob_hbm.1, f32[1536]{0:T(1024)} %bar_hbm.1, bf16[1024,1536]{1,0:T(8,128)(2,1)} %bitcast.3, ...), custom_call_target="tpu_custom_call" | custom-call | tf_op jit(solution)/shard_map/pallas_call | solution.py:671
  53.9 1.3 %shard_map.74 = f32[1536,256]{1,0:T(8,128)} custom-call(f32[1536,128]{1,0:T(8,128)S(1)} %get-tuple-element.9.left_ref, f32[1536,128]{1,0:T(8,128)S(1)} %get-tuple-element.10.right_ref, f32[1536,128]{1,0:T(8,128)S(1)} %get-tuple-element.11.h_ref, bf16[256,256]{1,0:T(8,128)(2,1)S(1)} %get-tuple-element.12.stack_ref), custom_call_target="tpu_custom_call" | custom-call | tf_op jit(solution)/shard_map/pallas_call | solution.py:724

commit v3 on v2

--- a/solution.py
+++ b/solution.py
@@ -90,6 +90,8 @@
                     left[tile] = left[tile] - factor * new_left[k:k + 1, :]
                     right[tile] = right[tile] - factor * new_right[k:k + 1, :]
             left[own], right[own] = new_left, new_right
+            if hook is not None:
+                hook(own)
         if base + per < tiles:
             upper = jnp.concatenate(left[base:base + per], axis=0)
             both = jnp.concatenate(
@@ -107,8 +109,6 @@
                 low = tile * SUB
                 left[tile] = left[tile] - change[low:low + SUB, :panel]
                 right[tile] = right[tile] - change[low:low + SUB, panel:]
-        if hook is not None:
-            hook(base // per)
     return jnp.concatenate(right, axis=0)
 
 
@@ -200,11 +200,11 @@
     b_ref, k_ref, base, load_sem, rest_sem, pv_row, pv_s, prob, bar_row, onehot,
     picked, xin, zsum, zin, columns, solved,
     fpick, fxin, fsum, fzin, fall,
-    bt, ct, tf, t_sum, t_in,
+    bt, ct, tf, t_sum, t_in, u_own, u_in, u_sum, u_all, mine,
     first_stack, out_half, in_half, steps, units, steps_in, units_in, h_first,
     rsx_send, rsz_send, ca_send, sa_send, rsz_recv, cx_recv, sx_recv,
     rsx_recv, cz_recv, sz_recv,
-    t_send, t_recv, c_send, c_recv, y_send, y_recv, g_send, g_recv,
+    t_send, t_recv, u_send, u_recv, c_send, c_recv, y_send, y_recv, g_send, g_recv,
 ):
     scen = lax.axis_index("scen")
     row = lax.axis_index("row")
@@ -332,7 +332,7 @@
 
     def ag_start(kind, p):
         held, send, zr, _ = kind
-        for peer in far:
+        for peer in near:
             go(remote(
                 held[p].at[row], held[p].at[row],
                 send.at[p], zr.at[p, z], {"row": 2 * peer + x},
@@ -463,24 +463,53 @@
             ct[p], solved[q].reshape(full, PANEL), preferred_element_type=F32
         ) + tf[p * PANEL:(p + 1) * PANEL, q * PANEL:(q + 1) * PANEL]
 
-    spans = [pl.ds(0, PANEL), pl.ds(PANEL, 2 * PANEL)]
-
-    def t_copy(which, index):
+    core = scen % 2
+    pair = {"scen": flip(scen, 1)}
+    bits = range(len(scen_bits))
+
+    def shared(own, into, sums, total, send, recv):
+        size = own.shape[0] // 2
+        here = pl.ds(pl.multiple_of(core * size, SUB), size)
+        there = pl.ds(pl.multiple_of((1 - core) * size, SUB), size)
+        final = len(scen_bits)
+
+        def copy(index):
+            return remote(
+                own.at[there, :] if index == 0 else sums.at[index - 1],
+                total.at[here, :] if index == final else into.at[index],
+                send.at[index], recv.at[index],
+                {"scen": flip(scen, scen_bits[index % final])},
+            )
+
+        def step(index):
+            copy(index).wait_recv()
+            before = own[here, :] if index == 0 else sums[index - 1]
+            sums[index] = before + into[index]
+            go(copy(index + 1))
+            if index + 1 == final:
+                total[here, :] = sums[index]
+
+        def end():
+            remote(
+                sums.at[0], total.at[there, :], send.at[final], recv.at[final], pair
+            ).wait_recv()
+
+        return copy, step, end
+
+    def t_copy(index):
         return remote(
-            t_sum.at[index, spans[which]], t_in.at[index, spans[which]],
-            t_send.at[which, index], t_recv.at[which, index],
+            t_sum.at[index], t_in.at[index], t_send.at[index], t_recv.at[index],
             {"scen": flip(scen, scen_bits[index])},
         )
 
-    def t_step(which, index):
-        t_copy(which, index).wait_recv()
-        t_sum[index + 1, spans[which]] = (
-            t_sum[index, spans[which]] + t_in[index, spans[which]]
-        )
+    def t_step(index):
+        t_copy(index).wait_recv()
+        t_sum[index + 1] = t_sum[index] + t_in[index]
         if index + 1 < len(scen_bits):
-            go(t_copy(which, index + 1))
-
-    core = scen % 2
+            go(t_copy(index + 1))
+
+    u_copy, u_step, u_end = shared(u_own, u_in, u_sum, u_all, u_send, u_recv)
+
     half = rows // 2
     chunk = half // PARTS
     parts = range(PARTS)
@@ -513,9 +542,11 @@
             ),
         )
 
-    def y_start(index, p, part, value):
+    def y_code(index, p, part, value):
         steps[index, p, part], unit = code(value)
         units[index, p, part] = jnp.broadcast_to(unit, units.shape[3:])
+
+    def y_go(index, p, part):
         for one in y_copies(index, p, part):
             go(one)
 
@@ -528,88 +559,133 @@
     def h_out(p):
         for part in parts:
             out_half[p, part] = term(1 - core, p, part)
+
+    def h_own(p):
+        for part in parts:
+            mine[part] = term(core, p, part)
+
+    def c_go(p):
+        for part in parts:
             go(c_copy(p, part))
 
     def h_join(p, part):
-        own = term(core, p, part)
-        c_copy(p, part).wait_recv()
-        y_start(0, p, part, own + in_half[p, part])
-
-    def y_step(p, part):
+        y_code(0, p, part, mine[part] + in_half[p, part])
+
+    def y_wait(p, part):
         for index in range(len(y_bits)):
             for one in y_copies(index, p, part):
                 one.wait_recv()
-            total = decode(
-                steps[index, p, part], units[index, p, part][0:1, :]
-            ) + decode(steps_in[index, p, part], units_in[index, p, part][0:1, :])
             if index + 1 < len(y_bits):
-                y_start(index + 1, p, part, total)
-            else:
-                done[p][place(core, part), :] = (
-                    total + base[place(core, part), p * PANEL:(p + 1) * PANEL]
-                )
-                go(g_copy(p, part, core))
+                y_code(index + 1, p, part, y_total(index, p, part))
+                y_go(index + 1, p, part)
+
+    def y_total(index, p, part):
+        return decode(
+            steps[index, p, part], units[index, p, part][0:1, :]
+        ) + decode(steps_in[index, p, part], units_in[index, p, part][0:1, :])
+
+    def h_end(p, part):
+        done[p][place(core, part), :] = (
+            y_total(len(y_bits) - 1, p, part)
+            + base[place(core, part), p * PANEL:(p + 1) * PANEL]
+        )
 
     ag_end(sols, 0)
     whole = t_block(0, 0)
-    t_sum[0, spans[0]] = 0.5 * (whole + whole.T)
-    go(t_copy(0, 0))
+    t_sum[0] = 0.5 * (whole + whole.T)
+    go(t_copy(0))
     for peer in near[-1:]:
         ag_pass(sols, 1, peer)
-    t_step(0, 0)
+    t_step(0)
     h_out(0)
-    h_join(0, 0)
+    c_go(0)
+    h_own(0)
+    for part in parts[:2]:
+        c_copy(0, part).wait_recv()
+        h_join(0, part)
+        y_go(0, 0, part)
+    for part in parts[2:]:
+        c_copy(0, part).wait_recv()
+        h_join(0, part)
     ag_end(sols, 1)
-    t_sum[0, PANEL:2 * PANEL] = 0.5 * (t_block(1, 0) + t_block(0, 1).T)
+    u_own[:PANEL, :] = 0.5 * (t_block(1, 0) + t_block(0, 1).T)
     whole = t_block(1, 1)
-    t_sum[0, 2 * PANEL:] = 0.5 * (whole + whole.T)
-    go(t_copy(1, 0))
-    for index in range(1, len(scen_bits)):
-        t_step(0, index)
-    last = len(scen_bits)
-
-    def hook_0(stage):
-        if stage == 0:
-            t_step(1, 0)
-            for part in parts[1:]:
-                h_join(0, part)
-        elif stage == 1:
+    u_own[PANEL:, :] = 0.5 * (whole + whole.T)
+    go(u_copy(0))
+    for index in bits[1:]:
+        t_step(index)
+
+    def hook_0(tile):
+        if tile == 1:
+            u_step(0)
+            for part in parts[2:]:
+                y_go(0, 0, part)
             h_out(1)
-        elif stage == 2:
+        elif tile == 4:
+            c_go(1)
+            h_own(1)
+        elif tile == 8:
+            for part in parts:
+                c_copy(1, part).wait_recv()
             for part in parts:
                 h_join(1, part)
-
-    inverse_0 = panel_inverse(t_sum[last, spans[0]], BLOCK, hook_0)
-    for index in range(1, len(scen_bits)):
-        t_step(1, index)
-    lower = product_t(t_sum[last, PANEL:2 * PANEL], wide(inverse_0))[0]
-    block = t_sum[last, 2 * PANEL:] - product_t(lower, wide(lower))[0]
+        elif tile == 11:
+            for part in parts:
+                y_go(0, 1, part)
+        elif tile == 14:
+            for index in bits[1:]:
+                u_step(index)
+
+    inverse_0 = panel_inverse(t_sum[len(scen_bits)], BLOCK, hook_0)
+    for part in parts[:2]:
+        y_wait(0, part)
+        h_end(0, part)
+        go(g_copy(0, part, core))
+    u_end()
+    lower = product_t(u_all[:PANEL, :], wide(inverse_0))[0]
+    block = u_all[PANEL:, :] - product_t(lower, wide(lower))[0]
 
     def g_end(p):
         some = done[p].at[pl.ds(0, half), :]
-        remote(
-            some, some, g_send.at[p], g_recv.at[p], {"scen": flip(scen, 1)}
-        ).wait_recv()
+        remote(some, some, g_send.at[p], g_recv.at[p], pair).wait_recv()
 
     def drop(which, part):
         left, right = product_t(h_first[place(which, part), :], first_stack[...])
         left_ref[place(which, part), :] = left
         right_ref[place(which, part), :] = right
 
-    def hook(stage):
-        if stage == 0:
+    def hook(tile):
+        if tile == 0:
             first_stack[...] = wide(inverse_0, product(lower, inverse_0))
+        elif tile == 2:
+            for part in parts[2:]:
+                y_wait(0, part)
+            for part in parts[2:]:
+                h_end(0, part)
+        elif tile == 4:
+            for part in parts[2:]:
+                go(g_copy(0, part, core))
             for part in parts:
-                y_step(0, part)
-        elif stage == 1:
+                drop(core, part)
+        elif tile == 8:
             g_end(0)
             for part in parts:
-                drop(core, part)
-        elif stage == 2:
-            for part in parts:
-                y_step(1, part)
-            for part in parts:
                 drop(1 - core, part)
+        elif tile == 11:
+            for part in parts[:2]:
+                y_wait(1, part)
+            for part in parts[:2]:
+                h_end(1, part)
+        elif tile == 13:
+            for part in parts[:2]:
+                go(g_copy(1, part, core))
+            for part in parts[2:]:
+                y_wait(1, part)
+            for part in parts[2:]:
+                h_end(1, part)
+        elif tile == 14:
+            for part in parts[2:]:
+                go(g_copy(1, part, core))
 
     stack_ref[...] = wide(panel_inverse(block, BLOCK, hook))
     g_end(1)
@@ -620,9 +696,10 @@
     for p in range(panels):
         drained(sol_of[p].at[pl.ds(0, n_row - 1)], sa_send.at[p])
         drained(done[p].at[pl.ds(0, half), :], g_send.at[p])
-    for which in range(2):
-        for index in range(len(scen_bits)):
-            t_copy(which, index).wait_send()
+    for index in bits:
+        t_copy(index).wait_send()
+    for index in range(len(scen_bits) + 1):
+        u_copy(index).wait_send()
     drained(out_half, c_send.at[0])
     drained(steps, y_send.at[0])
     drained(units, y_send.at[1])
@@ -696,8 +773,10 @@
             buf((n_row, frow, window), F32),
             buf((rows, full), BF16), buf((panels, PANEL, full), BF16),
             buf((window, window), F32),
-            buf((stages + 1, 3 * PANEL, PANEL), F32),
-            buf((stages, 3 * PANEL, PANEL), F32),
+            buf((stages + 1, PANEL, PANEL), F32), buf((stages, PANEL, PANEL), F32),
+            buf((2 * PANEL, PANEL), F32), buf((stages, PANEL, PANEL), F32),
+            buf((stages, PANEL, PANEL), F32), buf((2 * PANEL, PANEL), F32),
+            buf((PARTS, chunk, PANEL), F32),
             buf((4 * PANEL, 2 * PANEL), BF16),
             buf((panels, PARTS, chunk, PANEL), F32),
             buf((panels, PARTS, chunk, PANEL), F32),
@@ -706,7 +785,7 @@
             buf((rows, PANEL), F32),
             *[dma((panels + 1,))] * 3, dma((panels,)), *[dma((panels + 1,))] * 2,
             dma((panels,)), *[dma((panels + 1, nz))] * 2, dma((panels, nz)),
-            *[dma((2, stages))] * 2,
+            *[dma((stages,))] * 2, *[dma((stages + 1,))] * 2,
             dma((1,)), dma((panels, PARTS)),
             dma((2,)), dma((2, stages - 1, panels, PARTS)),
             *[dma((panels,))] * 2,

time: 55.3 us -> 52.4 us (0.948)
  Pallas kernels: 54.5 us -> 51.6 us
    pallas_call x1, Pallas kernels: 53.2 us -> 50.4 us  [per_device(): pl.pallas_call(functools.partial(schur_kernel, n_scen, n_row), out_shape=...]
where the time goes in v3:
time: 52.4 us; the launch traced here: 52.3 us
  Pallas kernels  51.6 us (98%)
  between operations  0.66 us (1%)
    pallas_call x1, Pallas kernels, per_device(): pl.pallas_call(functools.partial(schur_kernel, n_scen, n_row), out_shape=...  50.4 us
    pallas_call x1, Pallas kernels, per_device(): pl.pallas_call(functools.partial(last_kernel, pieces), out_shape=jax.Shap...  1.26 us

profile of v3, /device:TPU:0, one launch (start us, length us, event | category | flops | bytes accessed | tf_op | source)
XLA Modules:
  0.0 52.3 jit_solution(5539904234665870310)
XLA Ops:
  0.7 50.4 %shard_map.73 = (f32[1536,128]{1,0:T(8,128)S(1)}, f32[1536,128]{1,0:T(8,128)S(1)}, f32[1536,128]{1,0:T(8,128)S(1)}, bf16[256,256]{1,0:T(8,128)(2,1)S(1)}) custom-call(s32[1]{0:T(128)S(6)} %copy.8.asg, s32[1,256]{1,0:T(1,128)} %bitcast.5, f32[4]{0:T(128)} %prob_hbm.1, f32[1536]{0:T(1024)} %bar_hbm.1, bf16[1024,1536]{1,0:T(8,128)(2,1)} %bitcast.3, ...), custom_call_target="tpu_custom_call" | custom-call | tf_op jit(solution)/shard_map/pallas_call | solution.py:748
  51.0 1.3 %shard_map.74 = f32[1536,256]{1,0:T(8,128)} custom-call(f32[1536,128]{1,0:T(8,128)S(1)} %get-tuple-element.9.left_ref, f32[1536,128]{1,0:T(8,128)S(1)} %get-tuple-element.10.right_ref, f32[1536,128]{1,0:T(8,128)S(1)} %get-tuple-element.11.h_ref, bf16[256,256]{1,0:T(8,128)(2,1)S(1)} %get-tuple-element.12.stack_ref), custom_call_target="tpu_custom_call" | custom-call | tf_op jit(solution)/shard_map/pallas_call | solution.py:803

commit v4 on v3

--- a/solution.py
+++ b/solution.py
@@ -21,11 +21,8 @@
 TINY = 1e-30
 
 
-def small_factor(tile, first):
-    shape = tile.shape
-    spread = [
-        jnp.broadcast_to(tile[:, first + k:first + k + 1], shape) for k in range(SUB)
-    ]
+def small_factor(spread):
+    shape = spread[0].shape
     cell = {
         (i, k): jnp.broadcast_to(spread[k][i:i + 1, :], shape)
         for k in range(SUB) for i in range(k, SUB)
@@ -64,9 +61,32 @@
     right = [jnp.where(lane == sub + low, 1.0, 0.0) for low in range(0, panel, SUB)]
     per = size // SUB
     for base in range(0, tiles, per):
+        spread = {
+            (tile, own): [
+                jnp.broadcast_to(left[tile][:, at:at + 1], shape)
+                for at in range(own * SUB, own * SUB + SUB)
+            ]
+            for tile in range(base, base + per) for own in range(base, tile + 1)
+        }
         for own in range(base, base + per):
-            first = own * SUB
-            inverse = small_factor(left[own], first)
+            inverse = small_factor(spread[own, own])
+            rest = range(own + 1, base + per)
+            factors, lines = {}, {}
+            for tile in rest:
+                column = spread[tile, own]
+                for k in range(SUB):
+                    factor = column[0] * inverse[k, 0]
+                    for m in range(1, k + 1):
+                        factor = factor + column[m] * inverse[k, m]
+                    factors[tile, k] = factor
+                    for i in range(SUB):
+                        lines[tile, k, i] = jnp.broadcast_to(factor[i:i + 1, :], shape)
+                for across in range(own + 1, tile + 1):
+                    for i in range(SUB):
+                        change = factors[tile, 0] * lines[across, 0, i]
+                        for k in range(1, SUB):
+                            change = change + factors[tile, k] * lines[across, k, i]
+                        spread[tile, across][i] = spread[tile, across][i] - change
             new_left = new_right = None
             for k in range(SUB):
                 coeff = inverse[SUB - 1, k]
@@ -78,17 +98,10 @@
                 add_right = coeff * right[own][k:k + 1, :]
                 new_left = add_left if k == 0 else new_left + add_left
                 new_right = add_right if k == 0 else new_right + add_right
-            for tile in range(own + 1, base + per):
-                spread = [
-                    jnp.broadcast_to(left[tile][:, first + m:first + m + 1], shape)
-                    for m in range(SUB)
-                ]
+            for tile in rest:
                 for k in range(SUB):
-                    factor = spread[0] * inverse[k, 0]
-                    for m in range(1, k + 1):
-                        factor = factor + spread[m] * inverse[k, m]
-                    left[tile] = left[tile] - factor * new_left[k:k + 1, :]
-                    right[tile] = right[tile] - factor * new_right[k:k + 1, :]
+                    left[tile] = left[tile] - factors[tile, k] * new_left[k:k + 1, :]
+                    right[tile] = right[tile] - factors[tile, k] * new_right[k:k + 1, :]
             left[own], right[own] = new_left, new_right
             if hook is not None:
                 hook(own)

time: 52.4 us -> 52.1 us (level)
  no operation moved by 1% of the time
where the time goes in v4:
time: 52.1 us; the launch traced here: 51.9 us
  Pallas kernels  51.3 us (98%)
  between operations  0.66 us (1%)
    pallas_call x1, Pallas kernels, per_device(): pl.pallas_call(functools.partial(schur_kernel, n_scen, n_row), out_shape=...  50 us
    pallas_call x1, Pallas kernels, per_device(): pl.pallas_call(functools.partial(last_kernel, pieces), out_shape=jax.Shap...  1.26 us

profile of v4, /device:TPU:0, one launch (start us, length us, event | category | flops | bytes accessed | tf_op | source)
XLA Modules:
  0.0 51.9 jit_solution(13487675912970581589)
XLA Ops:
  0.7 50.0 %shard_map.73 = (f32[1536,128]{1,0:T(8,128)S(1)}, f32[1536,128]{1,0:T(8,128)S(1)}, f32[1536,128]{1,0:T(8,128)S(1)}, bf16[256,256]{1,0:T(8,128)(2,1)S(1)}) custom-call(s32[1]{0:T(128)S(6)} %copy.8.asg, s32[1,256]{1,0:T(1,128)} %bitcast.5, f32[4]{0:T(128)} %prob_hbm.1, f32[1536]{0:T(1024)} %bar_hbm.1, bf16[1024,1536]{1,0:T(8,128)(2,1)} %bitcast.3, ...), custom_call_target="tpu_custom_call" | custom-call | tf_op jit(solution)/shard_map/pallas_call | solution.py:761
  50.7 1.3 %shard_map.74 = f32[1536,256]{1,0:T(8,128)} custom-call(f32[1536,128]{1,0:T(8,128)S(1)} %get-tuple-element.9.left_ref, f32[1536,128]{1,0:T(8,128)S(1)} %get-tuple-element.10.right_ref, f32[1536,128]{1,0:T(8,128)S(1)} %get-tuple-element.11.h_ref, bf16[256,256]{1,0:T(8,128)(2,1)S(1)} %get-tuple-element.12.stack_ref), custom_call_target="tpu_custom_call" | custom-call | tf_op jit(solution)/shard_map/pallas_call | solution.py:816

commit v5 on v4

--- a/solution.py
+++ b/solution.py
@@ -43,7 +43,7 @@
             for m in range(j + 1, i):
                 total = total + lower[i, m] * inverse[m, j]
             inverse[i, j] = -(scale[i] * total)
-    return inverse
+    return inverse, scale, lower
 
 
 def split2(value):
@@ -69,24 +69,25 @@
             for tile in range(base, base + per) for own in range(base, tile + 1)
         }
         for own in range(base, base + per):
-            inverse = small_factor(spread[own, own])
+            inverse, scale, lower = small_factor(spread[own, own])
             rest = range(own + 1, base + per)
             factors, lines = {}, {}
             for tile in rest:
-                column = spread[tile, own]
+                column = list(spread[tile, own])
                 for k in range(SUB):
-                    factor = column[0] * inverse[k, 0]
-                    for m in range(1, k + 1):
-                        factor = factor + column[m] * inverse[k, m]
+                    factor = column[k] * scale[k]
+                    for m in range(k + 1, SUB):
+                        column[m] = column[m] - factor * lower[m, k]
                     factors[tile, k] = factor
                     for i in range(SUB):
                         lines[tile, k, i] = jnp.broadcast_to(factor[i:i + 1, :], shape)
                 for across in range(own + 1, tile + 1):
-                    for i in range(SUB):
-                        change = factors[tile, 0] * lines[across, 0, i]
-                        for k in range(1, SUB):
-                            change = change + factors[tile, k] * lines[across, k, i]
-                        spread[tile, across][i] = spread[tile, across][i] - change
+                    for k in range(SUB):
+                        for i in range(SUB):
+                            spread[tile, across][i] = (
+                                spread[tile, across][i]
+                                - factors[tile, k] * lines[across, k, i]
+                            )
             new_left = new_right = None
             for k in range(SUB):
                 coeff = inverse[SUB - 1, k]
@@ -380,6 +381,9 @@
     for p in range(1, panels):
         for peer in far + [z]:
             go(rsx(p, peer))
+    for peer in far + [z]:
+        pick(2 * peer + x)
+
     for one in small[1:]:
         one.wait()
     bar = split3(bar_row[...].reshape(1, rows))
@@ -413,9 +417,6 @@
     for peer in far + [z]:
         go(rsx(panels, peer))
 
-    for peer in far + [z]:
-        pick(2 * peer + x)
-
     for p in range(panels):
         rs_turn(p)
 
@@ -434,17 +435,16 @@
 
     rs_end(0)
     ag_start(cols, 0)
-    base[...] += onehot[...].astype(F32) * bsel
     tiles = rows // PANEL
-    lax.fori_loop(0, tiles // 2, turn, 0)
     ag_pass(cols, 0, near[0])
     rs_end(1)
     ag_start(cols, 1)
     rs_turn(panels)
     for peer in near[1:]:
         ag_pass(cols, 0, peer)
+    base[...] += onehot[...].astype(F32) * bsel
+    lax.fori_loop(0, tiles // 4, turn, 0)
     ag_pass(cols, 1, near[0])
-    lax.fori_loop(tiles // 2, tiles, turn, 0)
     k_load.wait()
     ag_end(cols, 0)
     solve(0)
@@ -453,6 +453,7 @@
     ag_start(cols, panels)
     for peer in near[1:]:
         ag_pass(cols, 1, peer)
+    lax.fori_loop(tiles // 4, tiles, turn, 0)
     side(0)
     ag_pass(sols, 0, near[0])
     ag_end(cols, 1)

time: 52.1 us -> 52.1 us (level)
  no operation moved by 1% of the time
where the time goes in v5:
time: 52.1 us; the launch traced here: 52 us
  Pallas kernels  51.3 us (98%)
  between operations  0.66 us (1%)
    pallas_call x1, Pallas kernels, per_device(): pl.pallas_call(functools.partial(schur_kernel, n_scen, n_row), out_shape=...  50 us
    pallas_call x1, Pallas kernels, per_device(): pl.pallas_call(functools.partial(last_kernel, pieces), out_shape=jax.Shap...  1.26 us

profile of v5, /device:TPU:0, one launch (start us, length us, event | category | flops | bytes accessed | tf_op | source)
XLA Modules:
  0.0 52.0 jit_solution(16915802824033658900)
XLA Ops:
  0.7 50.0 %shard_map.73 = (f32[1536,128]{1,0:T(8,128)S(1)}, f32[1536,128]{1,0:T(8,128)S(1)}, f32[1536,128]{1,0:T(8,128)S(1)}, bf16[256,256]{1,0:T(8,128)(2,1)S(1)}) custom-call(s32[1]{0:T(128)S(6)} %copy.8.asg, s32[1,256]{1,0:T(1,128)} %bitcast.5, f32[4]{0:T(128)} %prob_hbm.1, f32[1536]{0:T(1024)} %bar_hbm.1, bf16[1024,1536]{1,0:T(8,128)(2,1)} %bitcast.3, ...), custom_call_target="tpu_custom_call" | custom-call | tf_op jit(solution)/shard_map/pallas_call | solution.py:762
  50.7 1.3 %shard_map.74 = f32[1536,256]{1,0:T(8,128)} custom-call(f32[1536,128]{1,0:T(8,128)S(1)} %get-tuple-element.9.left_ref, f32[1536,128]{1,0:T(8,128)S(1)} %get-tuple-element.10.right_ref, f32[1536,128]{1,0:T(8,128)S(1)} %get-tuple-element.11.h_ref, bf16[256,256]{1,0:T(8,128)(2,1)S(1)} %get-tuple-element.12.stack_ref), custom_call_target="tpu_custom_call" | custom-call | tf_op jit(solution)/shard_map/pallas_call | solution.py:817
